TPU v7x, 32 devices: a whole 2x2x4 slice. The times are simulated.
32 devices in a mesh: stream: 2 (over y), batch: 16 (over z, x, core).
Axes of the slice: x: 2, y: 2, z: 4, core: 2. Of those that a mesh axis runs over, the one named last changes fastest.
Arguments:
- text_states: bfloat16 [128, 128, 768], P(('stream', 'batch')), may hold values from -6 to 6
- image_states: bfloat16 [128, 36, 1024], P(('stream', 'batch')), may hold values from -6 to 6
- caption_lengths: int32 [128], P(('stream', 'batch')), may hold values from 8 to 128, as said below
- region_counts: int32 [128], P(('stream', 'batch')), may hold values from 10 to 36, as said below
- text_cotangent: bfloat16 [128, 128, 768], P(('stream', 'batch')), may hold values from -6 to 6
- image_cotangent: bfloat16 [128, 36, 1024], P(('stream', 'batch')), may hold values from -6 to 6
- text_query: bfloat16 [768, 1024], P(('stream', 'batch')), may hold values from -0.21875 to 0.21875
- text_keyvalue: bfloat16 [768, 2048], P(('stream', 'batch')), may hold values from -0.21875 to 0.21875
- text_output: bfloat16 [1024, 768], P(('stream', 'batch')), may hold values from -0.75 to 0.75
- text_up: bfloat16 [768, 3072], P(('stream', 'batch')), may hold values from -0.21875 to 0.21875
- text_down: bfloat16 [3072, 768], P(('stream', 'batch')), may hold values from -0.109375 to 0.109375
- text_norm1_gain: bfloat16 [768], P(('stream', 'batch')), may hold values from 0.25 to 1.75
- text_norm1_bias: bfloat16 [768], P(('stream', 'batch')), may hold values from -1.1953125 to 1.1953125
- text_norm2_gain: bfloat16 [768], P(('stream', 'batch')), may hold values from 0.25 to 1.75
- text_norm2_bias: bfloat16 [768], P(('stream', 'batch')), may hold values from -1.1953125 to 1.1953125
- text_self_qkv: bfloat16 [768, 2304], P(('stream', 'batch')), may hold values from -0.21875 to 0.21875
- text_self_output: bfloat16 [768, 768], P(('stream', 'batch')), may hold values from -0.875 to 0.875
- text_norm0_gain: bfloat16 [768], P(('stream', 'batch')), may hold values from 0.25 to 1.75
- text_norm0_bias: bfloat16 [768], P(('stream', 'batch')), may hold values from -1.1953125 to 1.1953125
- image_query: bfloat16 [1024, 1024], P(('stream', 'batch')), may hold values from -0.1875 to 0.1875
- image_keyvalue: bfloat16 [1024, 2048], P(('stream', 'batch')), may hold values from -0.1875 to 0.1875
- image_output: bfloat16 [1024, 1024], P(('stream', 'batch')), may hold values from -0.75 to 0.75
- image_up: bfloat16 [1024, 1024], P(('stream', 'batch')), may hold values from -0.1875 to 0.1875
- image_down: bfloat16 [1024, 1024], P(('stream', 'batch')), may hold values from -0.1875 to 0.1875
- image_norm1_gain: bfloat16 [1024], P(('stream', 'batch')), may hold values from 0.25 to 1.75
- image_norm1_bias: bfloat16 [1024], P(('stream', 'batch')), may hold values from -1.1953125 to 1.1953125
- image_norm2_gain: bfloat16 [1024], P(('stream', 'batch')), may hold values from 0.25 to 1.75
- image_norm2_bias: bfloat16 [1024], P(('stream', 'batch')), may hold values from -1.1953125 to 1.1953125
- image_self_qkv: bfloat16 [1024, 3072], P(('stream', 'batch')), may hold values from -0.1875 to 0.1875
- image_self_output: bfloat16 [1024, 1024], P(('stream', 'batch')), may hold values from -0.5 to 0.5
- image_norm0_gain: bfloat16 [1024], P(('stream', 'batch')), may hold values from 0.25 to 1.75
- image_norm0_bias: bfloat16 [1024], P(('stream', 'batch')), may hold values from -1.1953125 to 1.1953125
Outputs:
- text_result: bfloat16 [128, 128, 768], P(('stream', 'batch'))
- image_result: bfloat16 [128, 36, 1024], P(('stream', 'batch'))
- text_states_grad: float32 [128, 128, 768], P(('stream', 'batch'))
- image_states_grad: float32 [128, 36, 1024], P(('stream', 'batch'))
- text_query_grad: float32 [768, 1024], P(('stream', 'batch'))
- text_keyvalue_grad: float32 [768, 2048], P(('stream', 'batch'))
- text_output_grad: float32 [1024, 768], P(('stream', 'batch'))
- text_up_grad: float32 [768, 3072], P(('stream', 'batch'))
- text_down_grad: float32 [3072, 768], P(('stream', 'batch'))
- text_norm1_gain_grad: float32 [768], P(('stream', 'batch'))
- text_norm1_bias_grad: float32 [768], P(('stream', 'batch'))
- text_norm2_gain_grad: float32 [768], P(('stream', 'batch'))
- text_norm2_bias_grad: float32 [768], P(('stream', 'batch'))
- text_self_qkv_grad: float32 [768, 2304], P(('stream', 'batch'))
- text_self_output_grad: float32 [768, 768], P(('stream', 'batch'))
- text_norm0_gain_grad: float32 [768], P(('stream', 'batch'))
- text_norm0_bias_grad: float32 [768], P(('stream', 'batch'))
- image_query_grad: float32 [1024, 1024], P(('stream', 'batch'))
- image_keyvalue_grad: float32 [1024, 2048], P(('stream', 'batch'))
- image_output_grad: float32 [1024, 1024], P(('stream', 'batch'))
- image_up_grad: float32 [1024, 1024], P(('stream', 'batch'))
- image_down_grad: float32 [1024, 1024], P(('stream', 'batch'))
- image_norm1_gain_grad: float32 [1024], P(('stream', 'batch'))
- image_norm1_bias_grad: float32 [1024], P(('stream', 'batch'))
- image_norm2_gain_grad: float32 [1024], P(('stream', 'batch'))
- image_norm2_bias_grad: float32 [1024], P(('stream', 'batch'))
- image_self_qkv_grad: float32 [1024, 3072], P(('stream', 'batch'))
- image_self_output_grad: float32 [1024, 1024], P(('stream', 'batch'))
- image_norm0_gain_grad: float32 [1024], P(('stream', 'batch'))
- image_norm0_bias_grad: float32 [1024], P(('stream', 'batch'))
Inputs may be any that keep to these rules, and one draw needn't show every extreme that they name: `caption_lengths`: each pair's caption length comes from one of three sets, short, medium or long; some pair fills all 128 slots. `region_counts`: some pair has all 36 regions.
All inputs are finite; a program needn't handle non-finite values.
Results may differ from a plain program's by a relative error of at most 0.02.
Values may be sent and summed in bfloat16 or wider, within the bound.
No kernel may reach another device: no remote copies, remote signals or barrier semaphores. Data moves between devices by JAX's collectives and lax.ppermute only.
A program may use at most 320 MiB of HBM per device.

v0:
```python
import jax
import jax.numpy as jnp
from jax import lax
from jax.sharding import Mesh
from jax.sharding import PartitionSpec as P

TEXT_HEADS = 12
IMAGE_HEADS = 8
HEADS = 8


EPS = 1e-05
NEG = -1e30


BLOCK = 256
ALL = ("stream", "ring", "core")
OUTER = ("stream", "ring")


def partner(block, axis, stride):
    count = lax.axis_size(axis)
    route = []
    for low in range(count):
        high = low | 1 << stride
        if high != low and high < count:
            route += [(low, high), (high, low)]
    return lax.ppermute(block, axis, route)


def layer_norm(values, gain, bias):
    mean = jnp.mean(values, axis=-1, keepdims=True)
    centred = values - mean
    spread = jnp.mean(centred * centred, axis=-1, keepdims=True)
    return centred * lax.rsqrt(spread + EPS) * gain + bias


def exact_gelu(values):
    return jax.nn.gelu(values, approximate=False)


def matmul(left, right):
    return jnp.dot(left, right, preferred_element_type=jnp.float32)


def matmul_back(grad, weight):
    return jnp.einsum("psn,wn->psw", grad, weight, preferred_element_type=jnp.float32)


def weight_grad(inputs, grad):
    return jnp.einsum("psw,psn->wn", inputs, grad, preferred_element_type=jnp.float32)


def score_layout(rows, count):
    if count < rows:
        return ("phkq", 2)
    return ("phqk", 3)


def attend(query, keys, values, live, heads):
    pairs, rows, inner = query.shape
    count = keys.shape[1]
    size = inner // heads
    scale = size ** (-0.5)
    layout, key_axis = score_layout(rows, count)
    heads_q = query.reshape(pairs, rows, heads, size)
    heads_k = keys.reshape(pairs, count, heads, size)
    heads_v = values.reshape(pairs, count, heads, size)
    scores = (
        jnp.einsum("pqhd,pkhd->" + layout, heads_q, heads_k, preferred_element_type=jnp.float32)
        * scale
    )
    if key_axis == 2:
        shown = live[:, None, :, None]
    else:
        shown = live[:, None, None, :]
    scores = jnp.where(shown, scores, NEG)
    highest = jnp.max(scores, axis=key_axis, keepdims=True)
    expo = jnp.exp(scores - highest)
    probs = expo / jnp.sum(expo, axis=key_axis, keepdims=True)
    low_probs = probs.astype(jnp.bfloat16)
    mixed = jnp.einsum(
        layout + ",pkhd->pqhd", low_probs, heads_v, preferred_element_type=jnp.float32
    )
    kept = (probs, low_probs, heads_q, heads_k, heads_v, layout, key_axis)
    return (mixed.reshape(pairs, rows, inner).astype(jnp.bfloat16), kept)


def attend_back(d_mixed, kept):
    probs, low_probs, heads_q, heads_k, heads_v, layout, key_axis = kept
    pairs, rows, heads, size = heads_q.shape
    count = heads_k.shape[1]
    scale = size ** (-0.5)
    d_heads = d_mixed.reshape(pairs, rows, heads, size)
    d_probs = jnp.einsum(
        "pqhd,pkhd->" + layout, d_heads, heads_v, preferred_element_type=jnp.float32
    )
    d_values = jnp.einsum(
        layout + ",pqhd->pkhd", low_probs, d_heads, preferred_element_type=jnp.float32
    )
    weighted = jnp.sum(d_probs * probs, axis=key_axis, keepdims=True)
    d_scores = (probs * (d_probs - weighted)).astype(jnp.bfloat16)
    d_query = (
        jnp.einsum(layout + ",pkhd->pqhd", d_scores, heads_k, preferred_element_type=jnp.float32)
        * scale
    )
    d_keys = (
        jnp.einsum(layout + ",pqhd->pkhd", d_scores, heads_q, preferred_element_type=jnp.float32)
        * scale
    )
    d_kv = jnp.concatenate(
        [d_keys.reshape(pairs, count, heads * size), d_values.reshape(pairs, count, heads * size)],
        axis=-1,
    )
    return (
        d_query.reshape(pairs, rows, heads * size).astype(jnp.bfloat16),
        d_kv.astype(jnp.bfloat16),
    )


def self_forward(states, weights, live, heads):
    width = states.shape[-1]
    qkv = matmul(states, weights[9]).astype(jnp.bfloat16)
    mixed, attn_kept = attend(
        qkv[..., :width], qkv[..., width : 2 * width], qkv[..., 2 * width :], live, heads
    )
    branch = matmul(mixed, weights[10])
    base, norm_back = jax.vjp(
        layer_norm,
        states.astype(jnp.float32) + branch,
        weights[11].astype(jnp.float32),
        weights[12].astype(jnp.float32),
    )
    return (base, (mixed, attn_kept, norm_back))


def self_backward(d_base, kept, states, weights):
    mixed, attn_kept, norm_back = kept
    d_pre, d_gain, d_bias = norm_back(d_base)
    d_branch = d_pre.astype(jnp.bfloat16)
    grad_self_output = weight_grad(mixed, d_branch)
    d_mixed = matmul_back(d_branch, weights[10]).astype(jnp.bfloat16)
    d_query, d_kv = attend_back(d_mixed, attn_kept)
    d_qkv = jnp.concatenate([d_query, d_kv], axis=-1)
    grad_self_qkv = weight_grad(states, d_qkv)
    d_states = d_pre + matmul_back(d_qkv, weights[9])
    return (d_states, (grad_self_qkv, grad_self_output, d_gain, d_bias))


def stream_forward(base, low_base, weights, key_values, live):
    inner = weights[0].shape[1]
    query = matmul(low_base, weights[0]).astype(jnp.bfloat16)
    mixed, attn_kept = attend(query, key_values[..., :inner], key_values[..., inner:], live, HEADS)
    branch = matmul(mixed, weights[2])
    norm_values = tuple((piece.astype(jnp.float32) for piece in weights[5:9]))
    hidden, first_norm = jax.vjp(layer_norm, base + branch, norm_values[0], norm_values[1])
    low_hidden = hidden.astype(jnp.bfloat16)
    active, gelu_back = jax.vjp(exact_gelu, matmul(low_hidden, weights[3]))
    low_active = active.astype(jnp.bfloat16)
    result, second_norm = jax.vjp(
        layer_norm, hidden + matmul(low_active, weights[4]), norm_values[2], norm_values[3]
    )
    kept = (low_base, mixed, attn_kept, first_norm, low_hidden, gelu_back, low_active, second_norm)
    return (result, kept)


def stream_backward(d_result, kept, weights):
    low_base, mixed, attn_kept, first_norm, low_hidden, gelu_back, low_active, second_norm = kept
    d_raw, d_gain_two, d_bias_two = second_norm(d_result)
    d_down_in = d_raw.astype(jnp.bfloat16)
    grad_down = weight_grad(low_active, d_down_in)
    d_gate = gelu_back(matmul_back(d_down_in, weights[4]))[0].astype(jnp.bfloat16)
    grad_up = weight_grad(low_hidden, d_gate)
    d_hidden = d_raw + matmul_back(d_gate, weights[3])
    d_sum, d_gain_one, d_bias_one = first_norm(d_hidden)
    d_branch = d_sum.astype(jnp.bfloat16)
    grad_output = weight_grad(mixed, d_branch)
    d_mixed = matmul_back(d_branch, weights[2]).astype(jnp.bfloat16)
    d_query, d_kv = attend_back(d_mixed, attn_kept)
    grad_query = weight_grad(low_base, d_query)
    d_base = d_sum + matmul_back(d_query, weights[0])
    grads = (
        grad_query,
        grad_output,
        grad_up,
        grad_down,
        d_gain_one,
        d_bias_one,
        d_gain_two,
        d_bias_two,
    )
    return (d_base, d_kv, grads)


def to_blocks(piece):
    rows, columns = piece.shape
    cut = piece.reshape(rows, columns // BLOCK, BLOCK)
    return cut.transpose(1, 0, 2).reshape(-1, BLOCK)


def vector_rows(vectors):
    rows = []
    for group in (vectors[:6], vectors[6:]):
        line = jnp.concatenate(group, axis=-1)
        width = line.shape[-1]
        lead = [(0, 0)] * (line.ndim - 1)
        rows.append(jnp.pad(line, lead + [(0, BLOCK - width)]))
    stacked = jnp.stack(rows, axis=-2)
    lead = [(0, 0)] * (stacked.ndim - 2)
    return jnp.pad(stacked, lead + [(0, 6), (0, 0)])


def gather_pack(pieces, vectors=None):
    parts = [to_blocks(piece) for piece in pieces]
    if vectors is not None:
        parts.append(vector_rows(vectors))
    packed = jnp.concatenate(parts, axis=0)
    whole = lax.all_gather(packed, ALL, axis=0, tiled=True)
    shards = whole.shape[0] // packed.shape[0]
    whole = whole.reshape(shards, packed.shape[0], BLOCK)
    full = []
    at = 0
    for piece in pieces:
        rows, columns = piece.shape
        count = columns // BLOCK
        part = whole[:, at : at + rows * count].reshape(shards, count, rows, BLOCK)
        full.append(part.transpose(0, 2, 1, 3).reshape(shards * rows, columns))
        at += rows * count
    if vectors is not None:
        for line, group in ((0, vectors[:6]), (1, vectors[6:])):
            size = group[0].shape[0]
            part = whole[:, at + line, : 6 * size].reshape(shards, 6, size)
            full += list(part.transpose(1, 0, 2).reshape(6, shards * size))
    return full


def scatter_pack(grads, vectors=None):
    shards = lax.axis_size(ALL)
    cores = lax.axis_size("core")
    outer = shards // cores
    core = lax.axis_index("core")

    def side(at):
        parts = []
        for grad in grads:
            rows = grad.shape[0] // shards
            count = grad.shape[1] // BLOCK
            cut = grad.astype(jnp.bfloat16).reshape(outer, cores, rows, count, BLOCK)
            half = lax.dynamic_index_in_dim(cut, at, axis=1, keepdims=False)
            parts.append(half.transpose(0, 2, 1, 3).reshape(outer, count * rows, BLOCK))
        if vectors is not None:
            lines = [vector.reshape(shards, -1) for vector in vectors]
            rows = vector_rows(lines).reshape(outer, cores, 8, BLOCK)
            half = lax.dynamic_index_in_dim(rows, at, axis=1, keepdims=False)
            parts.append(half.astype(jnp.bfloat16))
        return jnp.concatenate(parts, axis=1)

    given = lax.ppermute(side(cores - 1 - core), "core", [(c, cores - 1 - c) for c in range(cores)])
    total = side(core).astype(jnp.float32) + given.astype(jnp.float32)
    total = total.astype(jnp.bfloat16)
    own = lax.psum_scatter(total, OUTER, scatter_dimension=0, tiled=True)[0].astype(jnp.float32)
    result = []
    at = 0
    for grad in grads:
        rows = grad.shape[0] // shards
        count = grad.shape[1] // BLOCK
        part = own[at : at + rows * count].reshape(count, rows, BLOCK)
        result.append(part.transpose(1, 0, 2).reshape(rows, count * BLOCK))
        at += rows * count
    if vectors is not None:
        for line, group in ((0, vectors[:6]), (1, vectors[6:])):
            size = group[0].shape[0] // shards
            result += list(own[at + line, : 6 * size].reshape(6, size))
    return result


def local(
    text_states,
    image_states,
    caption_lengths,
    region_counts,
    text_cotangent,
    image_cotangent,
    text_query,
    text_keyvalue,
    text_output,
    text_up,
    text_down,
    text_norm1_gain,
    text_norm1_bias,
    text_norm2_gain,
    text_norm2_bias,
    text_self_qkv,
    text_self_output,
    text_norm0_gain,
    text_norm0_bias,
    image_query,
    image_keyvalue,
    image_output,
    image_up,
    image_down,
    image_norm1_gain,
    image_norm1_bias,
    image_norm2_gain,
    image_norm2_bias,
    image_self_qkv,
    image_self_output,
    image_norm0_gain,
    image_norm0_bias,
):
    home = partner((image_states, image_cotangent, region_counts), "stream", 0)
    image_states, image_cotangent, region_counts = home
    first = gather_pack(
        (
            text_self_qkv,
            image_self_qkv,
            text_self_output,
            image_self_output,
            text_keyvalue,
            image_keyvalue,
            text_query,
            image_query,
        ),
        (
            text_norm1_gain,
            text_norm1_bias,
            text_norm2_gain,
            text_norm2_bias,
            text_norm0_gain,
            text_norm0_bias,
            image_norm1_gain,
            image_norm1_bias,
            image_norm2_gain,
            image_norm2_bias,
            image_norm0_gain,
            image_norm0_bias,
        ),
    )
    second = gather_pack(
        (text_output, image_output, text_up, image_up, text_down, image_down)
    )
    text_norms = first[8:14]
    image_norms = first[14:20]
    text_weights = (
        (first[6], first[4], second[0], second[2], second[4])
        + tuple(text_norms[:4])
        + (first[0], first[2])
        + tuple(text_norms[4:])
    )
    image_weights = (
        (first[7], first[5], second[1], second[3], second[5])
        + tuple(image_norms[:4])
        + (first[1], first[3])
        + tuple(image_norms[4:])
    )
    pairs = text_states.shape[0]
    slots = text_states.shape[1]
    regions = image_states.shape[1]
    text_live = lax.broadcasted_iota(jnp.int32, (pairs, slots), 1) < caption_lengths[:, None]
    region_live = lax.broadcasted_iota(jnp.int32, (pairs, regions), 1) < region_counts[:, None]
    text_base, text_self_kept = self_forward(text_states, text_weights, text_live, TEXT_HEADS)
    image_base, image_self_kept = self_forward(
        image_states, image_weights, region_live, IMAGE_HEADS
    )
    low_text = text_base.astype(jnp.bfloat16)
    low_image = image_base.astype(jnp.bfloat16)
    text_kv = matmul(low_text, text_weights[1]).astype(jnp.bfloat16)
    image_kv = matmul(low_image, image_weights[1]).astype(jnp.bfloat16)
    text_result, text_kept = stream_forward(
        text_base, low_text, text_weights, image_kv, region_live
    )
    image_result, image_kept = stream_forward(
        image_base, low_image, image_weights, text_kv, text_live
    )
    image_result = partner(image_result.astype(jnp.bfloat16), "stream", 0)
    d_text_base, d_image_kv, text_grads = stream_backward(
        text_cotangent.astype(jnp.float32), text_kept, text_weights
    )
    d_image_base, d_text_kv, image_grads = stream_backward(
        image_cotangent.astype(jnp.float32), image_kept, image_weights
    )
    early = scatter_pack(
        (
            text_grads[1],
            image_grads[1],
            text_grads[2],
            image_grads[2],
            text_grads[3],
            image_grads[3],
        )
    )
    text_kv_grad = weight_grad(low_text, d_text_kv)
    image_kv_grad = weight_grad(low_image, d_image_kv)
    d_text_base = d_text_base + matmul_back(d_text_kv, text_weights[1])
    d_image_base = d_image_base + matmul_back(d_image_kv, image_weights[1])
    d_text, text_self_grads = self_backward(d_text_base, text_self_kept, text_states, text_weights)
    d_image, image_self_grads = self_backward(
        d_image_base, image_self_kept, image_states, image_weights
    )
    d_image = partner(d_image, "stream", 0)
    late = scatter_pack(
        (
            text_self_grads[0],
            image_self_grads[0],
            text_self_grads[1],
            image_self_grads[1],
            text_kv_grad,
            image_kv_grad,
            text_grads[0],
            image_grads[0],
        ),
        tuple(text_grads[4:8])
        + tuple(text_self_grads[2:4])
        + tuple(image_grads[4:8])
        + tuple(image_self_grads[2:4]),
    )
    return (
        text_result.astype(jnp.bfloat16),
        image_result,
        d_text,
        d_image,
        late[6],
        late[4],
        early[0],
        early[2],
        early[4],
        late[8],
        late[9],
        late[10],
        late[11],
        late[0],
        late[2],
        late[12],
        late[13],
        late[7],
        late[5],
        early[1],
        early[3],
        early[5],
        late[14],
        late[15],
        late[16],
        late[17],
        late[1],
        late[3],
        late[18],
        late[19],
    )


def split_mesh(mesh):
    streams = mesh.shape["stream"]
    batch = mesh.shape["batch"]
    cores = 2 if batch % 2 == 0 else 1
    return Mesh(mesh.devices.reshape(streams, batch // cores, cores), ALL)


def solution(mesh):
    rank_three = P(ALL, None, None)
    rank_two = P(ALL, None)
    rank_one = P(ALL)
    stream_specs = (rank_two,) * 5 + (rank_one,) * 4 + (rank_two,) * 2 + (rank_one,) * 2
    return jax.shard_map(
        local,
        mesh=split_mesh(mesh),
        in_specs=(rank_three,) * 2
        + (rank_one,) * 2
        + (rank_three,) * 2
        + stream_specs
        + stream_specs,
        out_specs=(rank_three,) * 4 + stream_specs + stream_specs,
        check_vma=False,
    )
```

profile of v0, /device:TPU:0, one launch (start us, length us, event | category | flops | bytes accessed | tf_op | source)
XLA Modules:
  0.0 1311.3 jit_solution(14463251177182313218)
XLA Ops:
  24.5 112.4 %all-gather.5.cloned.1.call-done = bf16[33792,256]{1,0:T(8,128)(2,1)} async-done(((bf16[1056,256]{1,0:T(8,128)(2,1)}), bf16[33792,256]{1,0:T(8,128)(2,1)}) %all-gather.5.cloned.1.call-update) | async-done | bytes 17301520 | tf_op jit(solution)/shard_map/all_gather | solution.py:218
  159.8 6.6 fusion.209
  170.7 9.5 reshape.1212
  180.2 8.5 copy.472
  188.6 12.5 reshape.1084
  207.5 80.7 %all-gather.3.cloned.1.call-done = bf16[47360,256]{1,0:T(8,128)(2,1)} async-done(((bf16[1480,256]{1,0:T(8,128)(2,1)}), bf16[47360,256]{1,0:T(8,128)(2,1)}) %all-gather.3.cloned.1.call-update) | async-done | bytes 24248336 | tf_op jit(solution)/shard_map/all_gather | solution.py:218
  375.9 11.5 copy.443
  387.3 12.3 reshape.1207
  524.7 7.6 reshape.1209
  545.8 6.9 fusion.29
  552.6 14.5 %multiply_convert_fusion = (bf16[4,128,3072]{2,1,0:T(8,128)(2,1)S(1)}, f32[4,128,3072]{2,1,0:T(8,128)S(1)}) fusion(f32[4,128,3072]{2,1,0:T(8,128)S(1)} %get-tuple-element.282, u8[128,3072]{1,0:T(8,128)(4,1)S(1)} %get-tuple-element.151, u8[128,3072]{1,0:T(8,128)(4,1)S(1)} %get-tuple-element.150), kind=kLoop, calls=%fused_computation.20 | loop fusion | flops 110100480 | bytes 16515072 | tf_op jit(solution)/shard_map/convert_element_type | solution.py:159
  577.7 6.3 add_convert_fusion.2
  685.7 9.2 reshape.1155
  700.9 11.6 reshape.1159
  712.5 7.2 constant_dynamic-slice_fusion.7
  825.1 8.7 copy.533
  833.8 12.2 reshape.1112
  860.8 7.9 add_convert_fusion.1
  884.2 18.5 %collective-permute-done.5 = bf16[16,1480,256]{2,1,0:T(8,128)(2,1)S(1)} collective-permute-done((bf16[16,1480,256]{2,1,0:T(8,128)(2,1)}, bf16[16,1480,256]{2,1,0:T(8,128)(2,1)S(1)}, u32[]{:S(2)}, u32[]{:S(2)}) %collective-permute-start.5) | collective-permute-done | bytes 12124192 | tf_op jit(solution)/shard_map/ppermute | solution.py:258
  902.7 6.6 add_convert_fusion
  909.4 8.5 reshape.1220
  931.7 17.0 %collective-permute-done.4 = f32[4,36,1024]{2,0,1:T(4,128)S(1)} collective-permute-done((f32[4,36,1024]{2,0,1:T(4,128)S(1)}, f32[4,36,1024]{2,0,1:T(4,128)S(1)}, u32[]{:S(2)}, u32[]{:S(2)}) %collective-permute-start.4) | collective-permute-done | bytes 589856 | tf_op jit(solution)/shard_map/ppermute | solution.py:28
  948.8 89.1 %reduce-scatter.5.cloned.1.call-done = bf16[1,1056,256]{2,1,0:T(8,128)(2,1)} async-done(((bf16[16,1056,256]{2,1,0:T(8,128)(2,1)}), bf16[1,1056,256]{2,1,0:T(8,128)(2,1)}) %reduce-scatter.5.cloned.1.call-update) | async-done | bytes 540688 | tf_op jit(solution)/shard_map/reduce_scatter | solution.py:261
  1044.8 248.6 %reduce-scatter.3.cloned.1.call-done = bf16[1,1480,256]{2,1,0:T(8,128)(2,1)} async-done(((bf16[16,1480,256]{2,1,0:T(8,128)(2,1)}), bf16[1,1480,256]{2,1,0:T(8,128)(2,1)}) %reduce-scatter.3.cloned.1.call-update) | async-done | bytes 757776 | tf_op jit(solution)/shard_map/reduce_scatter | solution.py:261
  (845 shorter events, 559.5 us)
Async XLA Ops:
  7.4 129.5 %all-gather.5.cloned.1.call-start = ((), (), s32[]{:S(2)}) async-start(), calls=%async_computation.3 | async-start | bytes 17842176 | tf_op jit(solution)/shard_map/all_gather | solution.py:218
  14.3 273.9 %all-gather.3.cloned.1.call-start = ((), (), s32[]{:S(2)}) async-start(), calls=%async_computation.2 | async-start | bytes 25006080 | tf_op jit(solution)/shard_map/all_gather | solution.py:218
  16.5 1021.4 %reduce-scatter.5.cloned.1.call-start = ((), (), s32[]{:S(2)}) async-start(), calls=%async_computation.5 | async-start | bytes 9191424 | tf_op jit(solution)/shard_map/reduce_scatter | solution.py:261
  16.6 7.3 collective-permute-start.1
  20.5 433.8 %collective-permute-start.3 = (bf16[4,36,1024]{2,1,0:T(8,128)(2,1)}, bf16[4,36,1024]{2,1,0:T(8,128)(2,1)}, u32[]{:S(2)}, u32[]{:S(2)}) collective-permute-start(bf16[4,36,1024]{2,1,0:T(8,128)(2,1)} %copy.492), channel_id=1, source_target_pairs={{0,16},{16,0},{1,17},{17,1},{2,18},{18,2},{3,19},{19,3},{4,20},{20... | collective-permute-start | bytes 884744 | tf_op jit(solution)/shard_map/ppermute | solution.py:28
  21.3 384.0 %collective-permute-start = (bf16[4,36,1024]{2,1,0:T(8,128)(2,1)}, bf16[4,36,1024]{2,1,0:T(8,128)(2,1)}, u32[]{:S(2)}, u32[]{:S(2)}) collective-permute-start(bf16[4,36,1024]{2,1,0:T(8,128)(2,1)} %copy.442), channel_id=1, source_target_pairs={{0,16},{16,0},{1,17},{17,1},{2,18},{18,2},{3,19},{19,3},{4,20},{20... | collective-permute-start | bytes 884744 | tf_op jit(solution)/shard_map/ppermute | solution.py:28
  387.3 12.3 copy-start.142
  405.3 20.7 %copy-start.44 = (bf16[4,16,8,8,128]{4,3,2,1,0:T(8,128)(2,1)}, bf16[4,16,8,8,128]{4,3,2,1,0:T(8,128)(2,1)S(1)}, u32[]{:S(2)}) copy-start(bf16[4,16,8,8,128]{4,3,2,1,0:T(8,128)(2,1)S(1)} %get-tuple-element.228) | copy-start | bytes 3145732
  421.8 12.8 copy-start.131
  422.0 12.6 copy-start.154
  443.3 20.0 %copy-start.28 = (f32[4,36,1024]{2,1,0:T(8,128)}, f32[4,36,1024]{2,1,0:T(8,128)S(1)}, u32[]{:S(2)}) copy-start(f32[4,36,1024]{2,1,0:T(8,128)S(1)} %get-tuple-element.291) | copy-start | bytes 1769476
  542.3 24.8 %slice-start.4 = ((s8[4718592]{0:T(1024)(128)(4,1)}), s8[4194304]{0:T(1024)(128)(4,1)S(1)}, s32[]{:S(2)}) async-start(s8[4718592]{0:T(1024)(128)(4,1)} %bitcast.630), calls=%async_computation.10 | async-start | bytes 8388608
  545.7 21.4 %slice-start.5 = ((s8[4718592]{0:T(1024)(128)(4,1)}), s8[524288]{0:T(1024)(128)(4,1)S(1)}, s32[]{:S(2)}) async-start(s8[4718592]{0:T(1024)(128)(4,1)} %bitcast.630), calls=%async_computation.11 | async-start | bytes 1048576
  572.5 11.5 slice-start.2
  595.6 27.3 %copy-start.181 = (f32[4,128]{1,0:T(4,128)}, f32[4,128]{1,0:T(4,128)S(1)}, u32[]{:S(2)}) copy-start(f32[4,128]{1,0:T(4,128)S(1)} %negate_multiply_fusion.6) | copy-start | bytes 6148
  662.4 13.1 copy-start.87
  662.4 17.6 %copy-start.72 = (bf16[1024,768]{1,0:T(8,128)(2,1)S(1)}, bf16[1024,768]{1,0:T(8,128)(2,1)}, u32[]{:S(2)}) copy-start(bf16[1024,768]{1,0:T(8,128)(2,1)} %bitcast_convert_fusion.11) | copy-start | bytes 4718596
  730.0 130.8 %collective-permute-start.6 = (bf16[16,1056,256]{2,1,0:T(8,128)(2,1)}, bf16[16,1056,256]{2,1,0:T(8,128)(2,1)}, u32[]{:S(2)}, u32[]{:S(2)}) collective-permute-start(bf16[16,1056,256]{2,1,0:T(8,128)(2,1)} %constant_dynamic-update-slice_fusion.44), channel_id=1, source_target_pairs={{0,1},{1,0},{2,3},{3,2},{4,5},{5,4},{6,7},{7,6},{8,9},{9,8},{10,11... | collective-permute-start | bytes 25952264 | tf_op jit(solution)/shard_map/ppermute | solution.py:258
  868.7 424.6 %reduce-scatter.3.cloned.1.call-start = ((), (), s32[]{:S(2)}) async-start(), calls=%async_computation.4 | async-start | bytes 12881920 | tf_op jit(solution)/shard_map/reduce_scatter | solution.py:261
  884.0 18.7 %collective-permute-start.5 = (bf16[16,1480,256]{2,1,0:T(8,128)(2,1)}, bf16[16,1480,256]{2,1,0:T(8,128)(2,1)S(1)}, u32[]{:S(2)}, u32[]{:S(2)}) collective-permute-start(bf16[16,1480,256]{2,1,0:T(8,128)(2,1)} %get-tuple-element.261), channel_id=1, source_target_pairs={{0,1},{1,0},{2,3},{3,2},{4,5},{5,4},{6,7},{7,6},{8,9},{9,8},{10,11... | collective-permute-start | bytes 36372488 | tf_op jit(solution)/shard_map/ppermute | solution.py:258
  909.3 9.8 copy-start.27
  909.3 9.8 copy-start.60
  917.9 12.9 collective-permute-start.2
  925.2 23.5 %collective-permute-start.4 = (f32[4,36,1024]{2,0,1:T(4,128)S(1)}, f32[4,36,1024]{2,0,1:T(4,128)S(1)}, u32[]{:S(2)}, u32[]{:S(2)}) collective-permute-start(f32[4,36,1024]{2,0,1:T(4,128)S(1)} %copy.529), channel_id=1, source_target_pairs={{0,16},{16,0},{1,17},{17,1},{2,18},{18,2},{3,19},{19,3},{4,20},{20... | collective-permute-start | bytes 1769480 | tf_op jit(solution)/shard_map/ppermute | solution.py:28
  (205 other events, 812.9 us)
Sparse Core Ops, SparseCore 0:
  14.4 122.4 all-gather.4
  140.4 147.7 all-gather.2
  868.9 168.9 reduce-scatter.4
  1040.1 253.2 reduce-scatter.2
where the time goes:
time: 1320 us; the launch traced here: 1310 us
  waiting for transfers between devices  568 us (43%)
  local copies, waits for them, and re-layouts  485 us (37%)
  matrix products  181 us (14%)
  other arithmetic  52.9 us (4%)
  between operations  17.4 us (1%)
    reduce_scatter x2, waiting for transfers between devices, scatter_pack(): lax.psum_scatter(total, OUTER, scatter_dimension=0, tiled=True)[0]  338 us
    all_gather x2, waiting for transfers between devices, gather_pack(): whole = lax.all_gather(packed, ALL, axis=0, tiled=True)  193 us
    reshape x14, local copies, waits for them, and re-layouts, gather_pack(): full.append(part.transpose(0, 2, 1, 3).reshape(shards * rows, columns))  84.4 us
    unnamed x503, local copies, waits for them, and re-layouts  69.1 us
    reshape x12, local copies, waits for them, and re-layouts, side(): cut = grad.astype(jnp.bfloat16).reshape(outer, cores, rows, count, BLOCK)  68.6 us
    transpose x14, local copies, waits for them, and re-layouts, gather_pack(): full.append(part.transpose(0, 2, 1, 3).reshape(shards * rows, columns))  62.1 us
    dynamic_slice x28, local copies, waits for them, and re-layouts, side(): half = lax.dynamic_index_in_dim(cut, at, axis=1, keepdims=False)  60.4 us
    dot_general x14, matrix products, matmul_back(): jnp.einsum('psn,wn->psw', grad, weight, preferred_element_type=jnp.float32)  51.2 us
  transfers between devices with their start and end apart: 11, of which 7 were waited for; matrix products, arithmetic and copies ran while one was open for 30% of the time, Pallas kernels for 0%

commit v1 on v0

--- a/solution.py
+++ b/solution.py
@@ -1,7 +1,6 @@
 import jax
 import jax.numpy as jnp
 from jax import lax
-from jax.sharding import Mesh
 from jax.sharding import PartitionSpec as P
 
 TEXT_HEADS = 12
@@ -13,9 +12,8 @@
 NEG = -1e30
 
 
-BLOCK = 256
-ALL = ("stream", "ring", "core")
-OUTER = ("stream", "ring")
+WIDTH = 768
+ALL = ("stream", "batch")
 
 
 def partner(block, axis, stride):
@@ -192,85 +190,106 @@
     return (d_base, d_kv, grads)
 
 
-def to_blocks(piece):
-    rows, columns = piece.shape
-    cut = piece.reshape(rows, columns // BLOCK, BLOCK)
-    return cut.transpose(1, 0, 2).reshape(-1, BLOCK)
-
-
-def vector_rows(vectors):
-    rows = []
-    for group in (vectors[:6], vectors[6:]):
-        line = jnp.concatenate(group, axis=-1)
-        width = line.shape[-1]
-        lead = [(0, 0)] * (line.ndim - 1)
-        rows.append(jnp.pad(line, lead + [(0, BLOCK - width)]))
-    stacked = jnp.stack(rows, axis=-2)
-    lead = [(0, 0)] * (stacked.ndim - 2)
-    return jnp.pad(stacked, lead + [(0, 6), (0, 0)])
-
-
-def gather_pack(pieces, vectors=None):
-    parts = [to_blocks(piece) for piece in pieces]
-    if vectors is not None:
-        parts.append(vector_rows(vectors))
+def lane_slabs(piece, width):
+    count = piece.shape[1] // width
+    return [piece[:, k * width : (k + 1) * width] for k in range(count)]
+
+
+def vector_rows(vectors, width):
+    line = jnp.concatenate(vectors, axis=-1)
+    short = -line.shape[-1] % width
+    line = jnp.pad(line, [(0, 0)] * (line.ndim - 1) + [(0, short)])
+    rows = line.reshape(line.shape[:-1] + (-1, width))
+    below = -rows.shape[-2] % 8
+    return jnp.pad(rows, [(0, 0)] * (rows.ndim - 2) + [(0, below), (0, 0)])
+
+
+def vector_cut(rows, sizes):
+    line = rows.reshape(rows.shape[:-2] + (-1,))
+    pieces = []
+    at = 0
+    for size in sizes:
+        pieces.append(line[..., at : at + size])
+        at += size
+    return pieces
+
+
+def gather_pack(groups, vectors=()):
+    parts = []
+    for group in groups:
+        joined = jnp.concatenate(group, axis=1)
+        short = -joined.shape[1] % WIDTH
+        parts += lane_slabs(jnp.pad(joined, ((0, 0), (0, short))), WIDTH)
+    if vectors:
+        parts.append(vector_rows(vectors, WIDTH))
     packed = jnp.concatenate(parts, axis=0)
     whole = lax.all_gather(packed, ALL, axis=0, tiled=True)
     shards = whole.shape[0] // packed.shape[0]
-    whole = whole.reshape(shards, packed.shape[0], BLOCK)
+    whole = whole.reshape(shards, packed.shape[0], WIDTH)
     full = []
     at = 0
-    for piece in pieces:
-        rows, columns = piece.shape
-        count = columns // BLOCK
-        part = whole[:, at : at + rows * count].reshape(shards, count, rows, BLOCK)
-        full.append(part.transpose(0, 2, 1, 3).reshape(shards * rows, columns))
-        at += rows * count
-    if vectors is not None:
-        for line, group in ((0, vectors[:6]), (1, vectors[6:])):
-            size = group[0].shape[0]
-            part = whole[:, at + line, : 6 * size].reshape(shards, 6, size)
-            full += list(part.transpose(1, 0, 2).reshape(6, shards * size))
+    for group in groups:
+        rows = group[0].shape[0]
+        columns = sum(piece.shape[1] for piece in group)
+        slabs = []
+        for _ in range(-(-columns // WIDTH)):
+            slabs.append(whole[:, at : at + rows].reshape(shards * rows, WIDTH))
+            at += rows
+        joined = jnp.concatenate(slabs, axis=1)
+        start = 0
+        for piece in group:
+            full.append(joined[:, start : start + piece.shape[1]])
+            start += piece.shape[1]
+    if vectors:
+        pieces = vector_cut(whole[:, at:], [vector.shape[0] for vector in vectors])
+        full += [piece.reshape(-1) for piece in pieces]
     return full
 
 
-def scatter_pack(grads, vectors=None):
+def halve(block, place, axis, bit):
+    mine = (lax.axis_index(axis) >> bit) & 1
+    route = [(at, at ^ (1 << bit)) for at in range(lax.axis_size(axis))]
+    keep = lax.dynamic_index_in_dim(block, mine, axis=place)
+    give = lax.dynamic_index_in_dim(block, 1 - mine, axis=place)
+    got = lax.ppermute(give, axis, route)
+    return keep.astype(jnp.float32) + got.astype(jnp.float32)
+
+
+def scatter_pack(groups, width, stream_first, vectors=()):
     shards = lax.axis_size(ALL)
-    cores = lax.axis_size("core")
-    outer = shards // cores
-    core = lax.axis_index("core")
-
-    def side(at):
-        parts = []
-        for grad in grads:
-            rows = grad.shape[0] // shards
-            count = grad.shape[1] // BLOCK
-            cut = grad.astype(jnp.bfloat16).reshape(outer, cores, rows, count, BLOCK)
-            half = lax.dynamic_index_in_dim(cut, at, axis=1, keepdims=False)
-            parts.append(half.transpose(0, 2, 1, 3).reshape(outer, count * rows, BLOCK))
-        if vectors is not None:
-            lines = [vector.reshape(shards, -1) for vector in vectors]
-            rows = vector_rows(lines).reshape(outer, cores, 8, BLOCK)
-            half = lax.dynamic_index_in_dim(rows, at, axis=1, keepdims=False)
-            parts.append(half.astype(jnp.bfloat16))
-        return jnp.concatenate(parts, axis=1)
-
-    given = lax.ppermute(side(cores - 1 - core), "core", [(c, cores - 1 - c) for c in range(cores)])
-    total = side(core).astype(jnp.float32) + given.astype(jnp.float32)
-    total = total.astype(jnp.bfloat16)
-    own = lax.psum_scatter(total, OUTER, scatter_dimension=0, tiled=True)[0].astype(jnp.float32)
+    bits = lax.axis_size("batch").bit_length() - 1
+    parts = []
+    for group in groups:
+        joined = group[0] if len(group) == 1 else jnp.concatenate(group, axis=1)
+        rows = joined.shape[0] // shards
+        for slab in lane_slabs(joined, width):
+            parts.append(slab.astype(jnp.bfloat16).reshape(shards, rows, width))
+    if vectors:
+        lines = [vector.reshape(shards, -1) for vector in vectors]
+        parts.append(vector_rows(lines, width).astype(jnp.bfloat16))
+    block = jnp.concatenate(parts, axis=1)
+    block = block.reshape((2,) * (bits + 1) + block.shape[1:])
+    order = [("batch", bit) for bit in range(bits)]
+    order.insert(1 if stream_first else 2, ("stream", 0))
+    for axis, bit in order:
+        place = 0 if axis == "stream" else bits - bit
+        block = halve(block.astype(jnp.bfloat16), place, axis, bit)
+    own = block.reshape(block.shape[-2:])
     result = []
     at = 0
-    for grad in grads:
-        rows = grad.shape[0] // shards
-        count = grad.shape[1] // BLOCK
-        part = own[at : at + rows * count].reshape(count, rows, BLOCK)
-        result.append(part.transpose(1, 0, 2).reshape(rows, count * BLOCK))
-        at += rows * count
-    if vectors is not None:
-        for line, group in ((0, vectors[:6]), (1, vectors[6:])):
-            size = group[0].shape[0] // shards
-            result += list(own[at + line, : 6 * size].reshape(6, size))
+    for group in groups:
+        rows = group[0].shape[0] // shards
+        slabs = []
+        for _ in range(sum(grad.shape[1] for grad in group) // width):
+            slabs.append(own[at : at + rows])
+            at += rows
+        joined = slabs[0] if len(slabs) == 1 else jnp.concatenate(slabs, axis=1)
+        start = 0
+        for grad in group:
+            result.append(joined[:, start : start + grad.shape[1]])
+            start += grad.shape[1]
+    if vectors:
+        result += vector_cut(own[at:], [vector.shape[0] // shards for vector in vectors])
     return result
 
 
@@ -310,16 +329,14 @@
 ):
     home = partner((image_states, image_cotangent, region_counts), "stream", 0)
     image_states, image_cotangent, region_counts = home
-    first = gather_pack(
+    qkv_t, so_t, qt, kvt, qkv_i, so_i, kvi, qi, *norms = gather_pack(
         (
-            text_self_qkv,
-            image_self_qkv,
-            text_self_output,
-            image_self_output,
-            text_keyvalue,
-            image_keyvalue,
-            text_query,
-            image_query,
+            (text_self_qkv,),
+            (text_self_output,),
+            (text_query, text_keyvalue),
+            (image_self_qkv,),
+            (image_self_output,),
+            (image_keyvalue, image_query),
         ),
         (
             text_norm1_gain,
@@ -336,23 +353,12 @@
             image_norm0_bias,
         ),
     )
-    second = gather_pack(
-        (text_output, image_output, text_up, image_up, text_down, image_down)
-    )
-    text_norms = first[8:14]
-    image_norms = first[14:20]
-    text_weights = (
-        (first[6], first[4], second[0], second[2], second[4])
-        + tuple(text_norms[:4])
-        + (first[0], first[2])
-        + tuple(text_norms[4:])
-    )
-    image_weights = (
-        (first[7], first[5], second[1], second[3], second[5])
-        + tuple(image_norms[:4])
-        + (first[1], first[3])
-        + tuple(image_norms[4:])
-    )
+    out_t, up_t, down_t, out_i, up_i, down_i = gather_pack(
+        ((text_output,), (text_up,), (text_down,), (image_output, image_up, image_down))
+    )
+    text_weights = (qt, kvt, out_t, up_t, down_t, *norms[:4], qkv_t, so_t, *norms[4:6])
+    image_weights = (qi, kvi, out_i, up_i, down_i, *norms[6:10], qkv_i, so_i, *norms[10:])
+    width = image_states.shape[2]
     pairs = text_states.shape[0]
     slots = text_states.shape[1]
     regions = image_states.shape[1]
@@ -379,18 +385,16 @@
     d_image_base, d_text_kv, image_grads = stream_backward(
         image_cotangent.astype(jnp.float32), image_kept, image_weights
     )
-    early = scatter_pack(
-        (
-            text_grads[1],
-            image_grads[1],
-            text_grads[2],
-            image_grads[2],
-            text_grads[3],
-            image_grads[3],
-        )
-    )
+    up_text, down_text = scatter_pack(((text_grads[2],), (text_grads[3],)), WIDTH, False)
+    up_image, down_image = scatter_pack(((image_grads[2],), (image_grads[3],)), width, True)
     text_kv_grad = weight_grad(low_text, d_text_kv)
     image_kv_grad = weight_grad(low_image, d_image_kv)
+    output_text, query_text, kv_text = scatter_pack(
+        ((text_grads[1],), (text_grads[0], text_kv_grad)), WIDTH, False
+    )
+    output_image, query_image, kv_image = scatter_pack(
+        ((image_grads[1],), (image_grads[0],), (image_kv_grad,)), width, True
+    )
     d_text_base = d_text_base + matmul_back(d_text_kv, text_weights[1])
     d_image_base = d_image_base + matmul_back(d_image_kv, image_weights[1])
     d_text, text_self_grads = self_backward(d_text_base, text_self_kept, text_states, text_weights)
@@ -398,61 +402,42 @@
         d_image_base, image_self_kept, image_states, image_weights
     )
     d_image = partner(d_image, "stream", 0)
-    late = scatter_pack(
-        (
-            text_self_grads[0],
-            image_self_grads[0],
-            text_self_grads[1],
-            image_self_grads[1],
-            text_kv_grad,
-            image_kv_grad,
-            text_grads[0],
-            image_grads[0],
-        ),
-        tuple(text_grads[4:8])
-        + tuple(text_self_grads[2:4])
-        + tuple(image_grads[4:8])
-        + tuple(image_self_grads[2:4]),
+    qkv_text, so_text, *text_vectors = scatter_pack(
+        ((text_self_grads[0],), (text_self_grads[1],)),
+        WIDTH,
+        False,
+        (*text_grads[4:8], *text_self_grads[2:4]),
+    )
+    qkv_image, so_image, *image_vectors = scatter_pack(
+        ((image_self_grads[0],), (image_self_grads[1],)),
+        width,
+        True,
+        (*image_grads[4:8], *image_self_grads[2:4]),
     )
     return (
         text_result.astype(jnp.bfloat16),
         image_result,
         d_text,
         d_image,
-        late[6],
-        late[4],
-        early[0],
-        early[2],
-        early[4],
-        late[8],
-        late[9],
-        late[10],
-        late[11],
-        late[0],
-        late[2],
-        late[12],
-        late[13],
-        late[7],
-        late[5],
-        early[1],
-        early[3],
-        early[5],
-        late[14],
-        late[15],
-        late[16],
-        late[17],
-        late[1],
-        late[3],
-        late[18],
-        late[19],
-    )
-
-
-def split_mesh(mesh):
-    streams = mesh.shape["stream"]
-    batch = mesh.shape["batch"]
-    cores = 2 if batch % 2 == 0 else 1
-    return Mesh(mesh.devices.reshape(streams, batch // cores, cores), ALL)
+        query_text,
+        kv_text,
+        output_text,
+        up_text,
+        down_text,
+        *text_vectors[:4],
+        qkv_text,
+        so_text,
+        *text_vectors[4:],
+        query_image,
+        kv_image,
+        output_image,
+        up_image,
+        down_image,
+        *image_vectors[:4],
+        qkv_image,
+        so_image,
+        *image_vectors[4:],
+    )
 
 
 def solution(mesh):
@@ -462,7 +447,7 @@
     stream_specs = (rank_two,) * 5 + (rank_one,) * 4 + (rank_two,) * 2 + (rank_one,) * 2
     return jax.shard_map(
         local,
-        mesh=split_mesh(mesh),
+        mesh=mesh,
         in_specs=(rank_three,) * 2
         + (rank_one,) * 2
         + (rank_three,) * 2

time: 1320 us -> 956 us (0.72)
  local copies, waits for them, and re-layouts: 485 us -> 184 us
  waiting for transfers between devices: 568 us -> 480 us
  other arithmetic: 52.9 us -> 72.5 us
  starting transfers between devices: 7.79 us -> 25.5 us
  matrix products: 181 us -> 166 us
    reduce_scatter x2 -> x0, waiting for transfers between devices: 338 us -> none  [scatter_pack(): lax.psum_scatter(total, OUTER, scatter_dimension=0, tiled=True)[0]]
    ppermute x2 -> x30, waiting for transfers between devices: 18.5 us -> 231 us  [halve(): got = lax.ppermute(give, axis, route)]
    reshape x60 -> x19, local copies, waits for them, and re-layouts: 167 us -> 8.01 us  [the longest x3 5.75 us: gather_pack(): slabs.append(whole[:, at:at + rows].reshape(shards * rows, WIDTH))]
    transpose x34 -> x0, local copies, waits for them, and re-layouts: 70.1 us -> none  [the longest x14 62.1 us: gather_pack(): full.append(part.transpose(0, 2, 1, 3).reshape(shards * rows, columns))]
    dynamic_slice x28 -> x29, local copies, waits for them, and re-layouts: 60.4 us -> 18.7 us  [halve(): give = lax.dynamic_index_in_dim(block, 1 - mine, axis=place)]
    all_gather x2, waiting for transfers between devices: 193 us -> 234 us  [gather_pack(): whole = lax.all_gather(packed, ALL, axis=0, tiled=True)]
    convert_element_type x3 -> x24, other arithmetic: 15.8 us -> 36.9 us  [scatter_pack(): block = halve(block.astype(jnp.bfloat16), place, axis, bit)]
    ppermute x2 -> x30, starting transfers between devices: 0.45 us -> 18.1 us  [halve(): got = lax.ppermute(give, axis, route)]
  transfers between devices with their start and end apart: 11 -> 37, of which waited for: 7 -> 20; matrix products, arithmetic and copies ran while one was open for 30% -> 18% of each run, Pallas kernels for 0% -> 0%
where the time goes in v1:
time: 956 us; the launch traced here: 946 us
  waiting for transfers between devices  480 us (50%)
  local copies, waits for them, and re-layouts  184 us (19%)
  matrix products  166 us (17%)
  other arithmetic  72.5 us (8%)
  starting transfers between devices  25.5 us (3%)
  between operations  17.7 us (2%)
    all_gather x2, waiting for transfers between devices, gather_pack(): whole = lax.all_gather(packed, ALL, axis=0, tiled=True)  234 us
    ppermute x30, waiting for transfers between devices, halve(): got = lax.ppermute(give, axis, route)  231 us
    unnamed x494, local copies, waits for them, and re-layouts  52.5 us
    dot_general x14, matrix products, matmul_back(): jnp.einsum('psn,wn->psw', grad, weight, preferred_element_type=jnp.float32)  45.3 us
    dot_general x14, matrix products, weight_grad(): jnp.einsum('psw,psn->wn', inputs, grad, preferred_element_type=jnp.float32)  37.6 us
    dot_general x14, matrix products, matmul(): return jnp.dot(left, right, preferred_element_type=jnp.float32)  37 us
    convert_element_type x24, other arithmetic, scatter_pack(): block = halve(block.astype(jnp.bfloat16), place, axis, bit)  36.9 us
    slice x5, local copies, waits for them, and re-layouts, gather_pack(): slabs.append(whole[:, at:at + rows].reshape(shards * rows, WIDTH))  34.3 us
  transfers between devices with their start and end apart: 37, of which 20 were waited for; matrix products, arithmetic and copies ran while one was open for 18% of the time, Pallas kernels for 0%

profile of v1, /device:TPU:0, one launch (start us, length us, event | category | flops | bytes accessed | tf_op | source)
XLA Modules:
  0.0 946.2 jit_solution(10395834751772643379)
XLA Ops:
  16.4 8.2 concatenate.187
  35.3 7.4 collective-permute-done.3
  43.4 92.6 %all-gather.5.cloned.1.call-done = bf16[11264,768]{1,0:T(8,128)(2,1)} async-done(((bf16[352,768]{1,0:T(8,128)(2,1)}), bf16[11264,768]{1,0:T(8,128)(2,1)}) %all-gather.5.cloned.1.call-update) | async-done | bytes 17301520 | tf_op jit(solution)/shard_map/all_gather | solution.py:226
  145.5 6.8 fusion.245
  152.3 141.4 %all-gather.3.cloned.1.call-done = bf16[16640,768]{1,0:T(8,128)(2,1)} async-done(((bf16[520,768]{1,0:T(8,128)(2,1)}), bf16[16640,768]{1,0:T(8,128)(2,1)}) %all-gather.3.cloned.1.call-update) | async-done | bytes 25559056 | tf_op jit(solution)/shard_map/all_gather | solution.py:226
  295.0 11.0 %fusion.243 = (bf16[32,32,768]{2,1,0:T(8,128)(2,1)S(1)}, bf16[32,32,768]{2,1,0:T(8,128)(2,1)}, bf16[32,32,768]{2,1,0:T(8,128)(2,1)}, bf16[32,32,768]{2,1,0:T(8,1...) fusion(bf16[32,520,768]{2,1,0:T(8,128)(2,1)} %bitcast.392), kind=kLoop, calls=%fused_computation.523 | loop fusion | bytes 31457280 | tf_op jit(solution)/shard_map/slice | solution.py:236
  306.6 7.0 fusion.244
  430.2 6.0 fusion.39
  436.2 14.1 %multiply_convert_fusion = (bf16[4,128,3072]{2,1,0:T(8,128)(2,1)S(1)}, f32[4,128,3072]{2,1,0:T(8,128)S(1)}) fusion(f32[4,128,3072]{2,1,0:T(8,128)S(1)} %get-tuple-element.271, u8[128,3072]{1,0:T(8,128)(4,1)S(1)} %get-tuple-element.121, u8[128,3072]{1,0:T(8,128)(4,1)S(1)} %get-tuple-element.120), kind=kLoop, calls=%fused_computation.24 | loop fusion | flops 110100480 | bytes 16515072 | tf_op jit(solution)/shard_map/convert_element_type | solution.py:157
  455.5 8.0 add_convert_fusion.4
  463.6 7.7 multiply_reduce_fusion.2
  620.7 18.1 %collective-permute-done.26 = bf16[1,2,2,2,1,64,1024]{6,5,4,3,2,1,0:T(8,128)(2,1)S(1)} collective-permute-done((bf16[1,2,2,2,1,64,1024]{6,5,4,3,2,1,0:T(8,128)(2,1)S(1)}, bf16[1,2,2,2,1,64,1024]{6,5,4,3,2,1,0:T(8,128)(2,1)S(1)}, u32[]{:S(2)}, u32[]{:S(2)}) %collective-permute-start.26) | collective-permute-done | bytes 1048608 | tf_op jit(solution)/shard_map/ppermute | solution.py:254
  647.1 8.4 collective-permute-done.4
  671.5 15.0 %collective-permute-done.16 = bf16[2,2,2,1,1,104,768]{6,5,4,3,2,1,0:T(8,128)(2,1)S(1)} collective-permute-done((bf16[2,2,2,1,1,104,768]{6,5,4,3,2,1,0:T(8,128)(2,1)S(1)}, bf16[2,2,2,1,1,104,768]{6,5,4,3,2,1,0:T(8,128)(2,1)S(1)}, u32[]{:S(2)}, u32[]{:S(2)}) %collective-permute-start.16) | collective-permute-done | bytes 1277984 | tf_op jit(solution)/shard_map/ppermute | solution.py:254
  703.6 6.1 add_convert_fusion.1
  734.1 85.1 %collective-permute-done.7 = bf16[1,2,2,1,1,128,768]{6,5,4,3,2,1,0:T(8,128)(2,1)S(1)} collective-permute-done((bf16[1,2,2,1,1,128,768]{6,5,4,3,2,1,0:T(8,128)(2,1)S(1)}, bf16[1,2,2,1,1,128,768]{6,5,4,3,2,1,0:T(8,128)(2,1)S(1)}, u32[]{:S(2)}, u32[]{:S(2)}) %collective-permute-start.7) | collective-permute-done | bytes 786464 | tf_op jit(solution)/shard_map/ppermute | solution.py:254
  820.9 8.3 collective-permute-done.8
  830.0 9.1 collective-permute-done.9
  849.5 19.2 %collective-permute-done.22 = bf16[1,2,2,1,1,128,1024]{6,5,4,3,2,1,0:T(8,128)(2,1)S(1)} collective-permute-done((bf16[1,2,2,1,1,128,1024]{6,5,4,3,2,1,0:T(8,128)(2,1)S(1)}, bf16[1,2,2,1,1,128,1024]{6,5,4,3,2,1,0:T(8,128)(2,1)S(1)}, u32[]{:S(2)}, u32[]{:S(2)}) %collective-permute-start.22) | collective-permute-done | bytes 1048608 | tf_op jit(solution)/shard_map/ppermute | solution.py:254
  873.0 6.9 collective-permute-done.23
  880.2 10.7 %collective-permute-done.32 = bf16[1,2,2,1,1,136,1024]{6,5,4,3,2,1,0:T(8,128)(2,1)S(1)} collective-permute-done((bf16[1,2,2,1,1,136,1024]{6,5,4,3,2,1,0:T(8,128)(2,1)S(1)}, bf16[1,2,2,1,1,136,1024]{6,5,4,3,2,1,0:T(8,128)(2,1)S(1)}, u32[]{:S(2)}, u32[]{:S(2)}) %collective-permute-start.32) | collective-permute-done | bytes 1114144 | tf_op jit(solution)/shard_map/ppermute | solution.py:254
  893.0 11.3 %collective-permute-done.33 = bf16[1,2,1,1,1,136,1024]{6,5,4,3,2,1,0:T(8,128)(2,1)S(1)} collective-permute-done((bf16[1,2,1,1,1,136,1024]{6,5,4,3,2,1,0:T(8,128)(2,1)S(1)}, bf16[1,2,1,1,1,136,1024]{6,5,4,3,2,1,0:T(8,128)(2,1)S(1)}, u32[]{:S(2)}, u32[]{:S(2)}) %collective-permute-start.33) | collective-permute-done | bytes 557088 | tf_op jit(solution)/shard_map/ppermute | solution.py:254
  905.4 12.2 %collective-permute-done.34 = bf16[1,1,1,1,1,136,1024]{6,5,4,3,2,1,0:T(8,128)(2,1)S(1)} collective-permute-done((bf16[1,1,1,1,1,136,1024]{6,5,4,3,2,1,0:T(8,128)(2,1)S(1)}, bf16[1,1,1,1,1,136,1024]{6,5,4,3,2,1,0:T(8,128)(2,1)S(1)}, u32[]{:S(2)}, u32[]{:S(2)}) %collective-permute-start.34) | collective-permute-done | bytes 278560 | tf_op jit(solution)/shard_map/ppermute | solution.py:254
  926.3 10.5 %collective-permute-done.14 = bf16[1,1,1,1,1,192,768]{6,5,4,3,2,1,0:T(8,128)(2,1)S(1)} collective-permute-done((bf16[1,1,1,1,1,192,768]{6,5,4,3,2,1,0:T(8,128)(2,1)S(1)}, bf16[1,1,1,1,1,192,768]{6,5,4,3,2,1,0:T(8,128)(2,1)S(1)}, u32[]{:S(2)}, u32[]{:S(2)}) %collective-permute-start.14) | collective-permute-done | bytes 294944 | tf_op jit(solution)/shard_map/ppermute | solution.py:254
  (840 shorter events, 397.2 us)
Async XLA Ops:
  7.3 128.8 %all-gather.5.cloned.1.call-start = ((), (), s32[]{:S(2)}) async-start(), calls=%async_computation.1 | async-start | bytes 17842176 | tf_op jit(solution)/shard_map/all_gather | solution.py:226
  16.4 277.3 %all-gather.3.cloned.1.call-start = ((), (), s32[]{:S(2)}) async-start(), calls=%async_computation | async-start | bytes 26357760 | tf_op jit(solution)/shard_map/all_gather | solution.py:226
  32.2 281.4 %collective-permute-start = (bf16[4,36,1024]{2,1,0:T(8,128)(2,1)S(1)}, bf16[4,36,1024]{2,1,0:T(8,128)(2,1)S(1)}, u32[]{:S(2)}, u32[]{:S(2)}) collective-permute-start(bf16[4,36,1024]{2,1,0:T(8,128)(2,1)S(1)} %copy.203), channel_id=1, source_target_pairs={{0,16},{16,0},{1,17},{17,1},{2,18},{18,2},{3,19},{19,3},{4,20},{20... | collective-permute-start | bytes 884744 | tf_op jit(solution)/shard_map/ppermute | solution.py:26
  538.0 101.7 %collective-permute-start.2 = (bf16[4,36,1024]{2,1,0:T(8,128)(2,1)}, bf16[4,36,1024]{2,1,0:T(8,128)(2,1)}, u32[]{:S(2)}, u32[]{:S(2)}) collective-permute-start(bf16[4,36,1024]{2,1,0:T(8,128)(2,1)} %get-tuple-element.206), channel_id=1, source_target_pairs={{0,16},{16,0},{1,17},{17,1},{2,18},{18,2},{3,19},{19,3},{4,20},{20... | collective-permute-start | bytes 884744 | tf_op jit(solution)/shard_map/ppermute | solution.py:26
  544.9 62.4 %collective-permute-start.25 = (bf16[2,2,2,2,1,64,1024]{6,5,4,3,2,1,0:T(8,128)(2,1)}, bf16[2,2,2,2,1,64,1024]{6,5,4,3,2,1,0:T(8,128)(2,1)}, u32[]{:S(2)}, u32[]{:S(2)}) collective-permute-start(bf16[2,2,2,2,1,64,1024]{6,5,4,3,2,1,0:T(8,128)(2,1)} %fusion.18), channel_id=1, source_target_pairs={{0,1},{1,0},{2,3},{3,2},{4,5},{5,4},{6,7},{7,6},{8,9},{9,8},{10,11... | collective-permute-start | bytes 6291464 | tf_op jit(solution)/shard_map/ppermute | solution.py:254
  587.1 108.1 %collective-permute-start.20 = (bf16[2,2,2,2,1,128,1024]{6,5,4,3,2,1,0:T(8,128)(2,1)}, bf16[2,2,2,2,1,128,1024]{6,5,4,3,2,1,0:T(8,128)(2,1)}, u32[]{:S(2)}, u32[]{:S(2)}) collective-permute-start(bf16[2,2,2,2,1,128,1024]{6,5,4,3,2,1,0:T(8,128)(2,1)} %constant_dynamic-slice_fusion.13), channel_id=1, source_target_pairs={{0,1},{1,0},{2,3},{3,2},{4,5},{5,4},{6,7},{7,6},{8,9},{9,8},{10,11... | collective-permute-start | bytes 12582920 | tf_op jit(solution)/shard_map/ppermute | solution.py:254
  593.5 68.0 %collective-permute-start.5 = (bf16[2,2,2,2,1,128,768]{6,5,4,3,2,1,0:T(8,128)(2,1)}, bf16[2,2,2,2,1,128,768]{6,5,4,3,2,1,0:T(8,128)(2,1)}, u32[]{:S(2)}, u32[]{:S(2)}) collective-permute-start(bf16[2,2,2,2,1,128,768]{6,5,4,3,2,1,0:T(8,128)(2,1)} %constant_dynamic-slice_fusion.28), channel_id=1, source_target_pairs={{0,1},{1,0},{2,3},{3,2},{4,5},{5,4},{6,7},{7,6},{8,9},{9,8},{10,11... | collective-permute-start | bytes 9437192 | tf_op jit(solution)/shard_map/ppermute | solution.py:254
  598.5 41.9 %collective-permute-start.15 = (bf16[2,2,2,2,1,104,768]{6,5,4,3,2,1,0:T(8,128)(2,1)}, bf16[2,2,2,2,1,104,768]{6,5,4,3,2,1,0:T(8,128)(2,1)}, u32[]{:S(2)}, u32[]{:S(2)}) collective-permute-start(bf16[2,2,2,2,1,104,768]{6,5,4,3,2,1,0:T(8,128)(2,1)} %constant_dynamic-slice_fusion.18), channel_id=1, source_target_pairs={{0,1},{1,0},{2,3},{3,2},{4,5},{5,4},{6,7},{7,6},{8,9},{9,8},{10,11... | collective-permute-start | bytes 7667720 | tf_op jit(solution)/shard_map/ppermute | solution.py:254
  613.2 25.6 %collective-permute-start.26 = (bf16[1,2,2,2,1,64,1024]{6,5,4,3,2,1,0:T(8,128)(2,1)S(1)}, bf16[1,2,2,2,1,64,1024]{6,5,4,3,2,1,0:T(8,128)(2,1)S(1)}, u32[]{:S(2)}, u32[]{:S(2)}) collective-permute-start(bf16[1,2,2,2,1,64,1024]{6,5,4,3,2,1,0:T(8,128)(2,1)S(1)} %constant_dynamic-slice_fusion.8), channel_id=1, source_target_pairs={{0,16},{16,0},{1,17},{17,1},{2,18},{18,2},{3,19},{19,3},{4,20},{20... | collective-permute-start | bytes 3145736 | tf_op jit(solution)/shard_map/ppermute | solution.py:254
  638.8 64.8 %collective-permute-start.30 = (bf16[2,2,2,2,1,136,1024]{6,5,4,3,2,1,0:T(8,128)(2,1)}, bf16[2,2,2,2,1,136,1024]{6,5,4,3,2,1,0:T(8,128)(2,1)}, u32[]{:S(2)}, u32[]{:S(2)}) collective-permute-start(bf16[2,2,2,2,1,136,1024]{6,5,4,3,2,1,0:T(8,128)(2,1)} %constant_dynamic-slice_fusion.4), channel_id=1, source_target_pairs={{0,1},{1,0},{2,3},{3,2},{4,5},{5,4},{6,7},{7,6},{8,9},{9,8},{10,11... | collective-permute-start | bytes 13369352 | tf_op jit(solution)/shard_map/ppermute | solution.py:254
  639.7 15.8 %collective-permute-start.4 = (f32[4,36,1024]{2,0,1:T(4,128)S(1)}, f32[4,36,1024]{2,0,1:T(4,128)S(1)}, u32[]{:S(2)}, u32[]{:S(2)}) collective-permute-start(f32[4,36,1024]{2,0,1:T(4,128)S(1)} %copy-done.122), channel_id=1, source_target_pairs={{0,16},{16,0},{1,17},{17,1},{2,18},{18,2},{3,19},{19,3},{4,20},{20... | collective-permute-start | bytes 1769480 | tf_op jit(solution)/shard_map/ppermute | solution.py:26
  640.3 15.2 %collective-permute-start.27 = (bf16[1,2,2,1,1,64,1024]{6,5,4,3,2,1,0:T(8,128)(2,1)S(1)}, bf16[1,2,2,1,1,64,1024]{6,5,4,3,2,1,0:T(8,128)(2,1)S(1)}, u32[]{:S(2)}, u32[]{:S(2)}) collective-permute-start(bf16[1,2,2,1,1,64,1024]{6,5,4,3,2,1,0:T(8,128)(2,1)S(1)} %constant_dynamic-slice_fusion.7), channel_id=1, source_target_pairs={{0,2},{1,3},{2,0},{3,1},{4,6},{5,7},{6,4},{7,5},{8,10},{9,11},{10,... | collective-permute-start | bytes 1572872 | tf_op jit(solution)/shard_map/ppermute | solution.py:254
  655.5 65.4 %collective-permute-start.10 = (bf16[2,2,2,2,1,192,768]{6,5,4,3,2,1,0:T(8,128)(2,1)}, bf16[2,2,2,2,1,192,768]{6,5,4,3,2,1,0:T(8,128)(2,1)}, u32[]{:S(2)}, u32[]{:S(2)}) collective-permute-start(bf16[2,2,2,2,1,192,768]{6,5,4,3,2,1,0:T(8,128)(2,1)} %constant_dynamic-slice_fusion.23), channel_id=1, source_target_pairs={{0,1},{1,0},{2,3},{3,2},{4,5},{5,4},{6,7},{7,6},{8,9},{9,8},{10,11... | collective-permute-start | bytes 14155784 | tf_op jit(solution)/shard_map/ppermute | solution.py:254
  655.5 31.0 %collective-permute-start.16 = (bf16[2,2,2,1,1,104,768]{6,5,4,3,2,1,0:T(8,128)(2,1)S(1)}, bf16[2,2,2,1,1,104,768]{6,5,4,3,2,1,0:T(8,128)(2,1)S(1)}, u32[]{:S(2)}, u32[]{:S(2)}) collective-permute-start(bf16[2,2,2,1,1,104,768]{6,5,4,3,2,1,0:T(8,128)(2,1)S(1)} %constant_dynamic-slice_fusion.17), channel_id=1, source_target_pairs={{0,2},{1,3},{2,0},{3,1},{4,6},{5,7},{6,4},{7,5},{8,10},{9,11},{10,... | collective-permute-start | bytes 3833864 | tf_op jit(solution)/shard_map/ppermute | solution.py:254
  670.0 49.7 %collective-permute-start.6 = (bf16[2,2,2,1,1,128,768]{6,5,4,3,2,1,0:T(8,128)(2,1)}, bf16[2,2,2,1,1,128,768]{6,5,4,3,2,1,0:T(8,128)(2,1)S(1)}, u32[]{:S(2)}, u32[]{:S(2)}) collective-permute-start(bf16[2,2,2,1,1,128,768]{6,5,4,3,2,1,0:T(8,128)(2,1)} %constant_dynamic-slice_fusion.27), channel_id=1, source_target_pairs={{0,2},{1,3},{2,0},{3,1},{4,6},{5,7},{6,4},{7,5},{8,10},{9,11},{10,... | collective-permute-start | bytes 4718600 | tf_op jit(solution)/shard_map/ppermute | solution.py:254
  693.9 19.1 %collective-permute-start.17 = (bf16[1,2,2,1,1,104,768]{6,5,4,3,2,1,0:T(8,128)(2,1)S(1)}, bf16[1,2,2,1,1,104,768]{6,5,4,3,2,1,0:T(8,128)(2,1)}, u32[]{:S(2)}, u32[]{:S(2)}) collective-permute-start(bf16[1,2,2,1,1,104,768]{6,5,4,3,2,1,0:T(8,128)(2,1)S(1)} %constant_dynamic-slice_fusion.16), channel_id=1, source_target_pairs={{0,16},{16,0},{1,17},{17,1},{2,18},{18,2},{3,19},{19,3},{4,20},{20... | collective-permute-start | bytes 1916936 | tf_op jit(solution)/shard_map/ppermute | solution.py:254
  702.1 137.0 %collective-permute-start.21 = (bf16[1,2,2,2,1,128,1024]{6,5,4,3,2,1,0:T(8,128)(2,1)}, bf16[1,2,2,2,1,128,1024]{6,5,4,3,2,1,0:T(8,128)(2,1)}, u32[]{:S(2)}, u32[]{:S(2)}) collective-permute-start(bf16[1,2,2,2,1,128,1024]{6,5,4,3,2,1,0:T(8,128)(2,1)} %constant_dynamic-slice_fusion.12), channel_id=1, source_target_pairs={{0,16},{16,0},{1,17},{17,1},{2,18},{18,2},{3,19},{19,3},{4,20},{20... | collective-permute-start | bytes 6291464 | tf_op jit(solution)/shard_map/ppermute | solution.py:254
  712.4 132.3 %collective-permute-start.31 = (bf16[1,2,2,2,1,136,1024]{6,5,4,3,2,1,0:T(8,128)(2,1)}, bf16[1,2,2,2,1,136,1024]{6,5,4,3,2,1,0:T(8,128)(2,1)}, u32[]{:S(2)}, u32[]{:S(2)}) collective-permute-start(bf16[1,2,2,2,1,136,1024]{6,5,4,3,2,1,0:T(8,128)(2,1)} %constant_dynamic-slice_fusion.3), channel_id=1, source_target_pairs={{0,16},{16,0},{1,17},{17,1},{2,18},{18,2},{3,19},{19,3},{4,20},{20... | collective-permute-start | bytes 6684680 | tf_op jit(solution)/shard_map/ppermute | solution.py:254
  720.2 99.0 %collective-permute-start.7 = (bf16[1,2,2,1,1,128,768]{6,5,4,3,2,1,0:T(8,128)(2,1)S(1)}, bf16[1,2,2,1,1,128,768]{6,5,4,3,2,1,0:T(8,128)(2,1)S(1)}, u32[]{:S(2)}, u32[]{:S(2)}) collective-permute-start(bf16[1,2,2,1,1,128,768]{6,5,4,3,2,1,0:T(8,128)(2,1)S(1)} %constant_dynamic-slice_fusion.26), channel_id=1, source_target_pairs={{0,16},{16,0},{1,17},{17,1},{2,18},{18,2},{3,19},{19,3},{4,20},{20... | collective-permute-start | bytes 2359304 | tf_op jit(solution)/shard_map/ppermute | solution.py:254
  728.3 141.7 %collective-permute-start.11 = (bf16[2,2,2,1,1,192,768]{6,5,4,3,2,1,0:T(8,128)(2,1)}, bf16[2,2,2,1,1,192,768]{6,5,4,3,2,1,0:T(8,128)(2,1)}, u32[]{:S(2)}, u32[]{:S(2)}) collective-permute-start(bf16[2,2,2,1,1,192,768]{6,5,4,3,2,1,0:T(8,128)(2,1)} %constant_dynamic-slice_fusion.22), channel_id=1, source_target_pairs={{0,2},{1,3},{2,0},{3,1},{4,6},{5,7},{6,4},{7,5},{8,10},{9,11},{10,... | collective-permute-start | bytes 7077896 | tf_op jit(solution)/shard_map/ppermute | solution.py:254
  842.7 26.1 %collective-permute-start.22 = (bf16[1,2,2,1,1,128,1024]{6,5,4,3,2,1,0:T(8,128)(2,1)S(1)}, bf16[1,2,2,1,1,128,1024]{6,5,4,3,2,1,0:T(8,128)(2,1)S(1)}, u32[]{:S(2)}, u32[]{:S(2)}) collective-permute-start(bf16[1,2,2,1,1,128,1024]{6,5,4,3,2,1,0:T(8,128)(2,1)S(1)} %constant_dynamic-slice_fusion.11), channel_id=1, source_target_pairs={{0,2},{1,3},{2,0},{3,1},{4,6},{5,7},{6,4},{7,5},{8,10},{9,11},{10,... | collective-permute-start | bytes 3145736 | tf_op jit(solution)/shard_map/ppermute | solution.py:254
  848.0 43.0 %collective-permute-start.32 = (bf16[1,2,2,1,1,136,1024]{6,5,4,3,2,1,0:T(8,128)(2,1)S(1)}, bf16[1,2,2,1,1,136,1024]{6,5,4,3,2,1,0:T(8,128)(2,1)S(1)}, u32[]{:S(2)}, u32[]{:S(2)}) collective-permute-start(bf16[1,2,2,1,1,136,1024]{6,5,4,3,2,1,0:T(8,128)(2,1)S(1)} %constant_dynamic-slice_fusion.2), channel_id=1, source_target_pairs={{0,2},{1,3},{2,0},{3,1},{4,6},{5,7},{6,4},{7,5},{8,10},{9,11},{10,... | collective-permute-start | bytes 3342344 | tf_op jit(solution)/shard_map/ppermute | solution.py:254
  872.3 32.4 %collective-permute-start.12 = (bf16[1,2,2,1,1,192,768]{6,5,4,3,2,1,0:T(8,128)(2,1)S(1)}, bf16[1,2,2,1,1,192,768]{6,5,4,3,2,1,0:T(8,128)(2,1)S(1)}, u32[]{:S(2)}, u32[]{:S(2)}) collective-permute-start(bf16[1,2,2,1,1,192,768]{6,5,4,3,2,1,0:T(8,128)(2,1)S(1)} %constant_dynamic-slice_fusion.21), channel_id=1, source_target_pairs={{0,16},{16,0},{1,17},{17,1},{2,18},{18,2},{3,19},{19,3},{4,20},{20... | collective-permute-start | bytes 3538952 | tf_op jit(solution)/shard_map/ppermute | solution.py:254
  905.1 18.8 %collective-permute-start.13 = (bf16[1,2,1,1,1,192,768]{6,5,4,3,2,1,0:T(8,128)(2,1)S(1)}, bf16[1,2,1,1,1,192,768]{6,5,4,3,2,1,0:T(8,128)(2,1)S(1)}, u32[]{:S(2)}, u32[]{:S(2)}) collective-permute-start(bf16[1,2,1,1,1,192,768]{6,5,4,3,2,1,0:T(8,128)(2,1)S(1)} %constant_dynamic-slice_fusion.20), channel_id=1, source_target_pairs={{0,4},{1,5},{2,6},{3,7},{4,0},{5,1},{6,2},{7,3},{8,12},{9,13},{10,... | collective-permute-start | bytes 1769480 | tf_op jit(solution)/shard_map/ppermute | solution.py:254
  (234 other events, 2369.2 us)
Sparse Core Ops, SparseCore 0:
  16.5 119.5 all-gather.4
  139.5 154.1 all-gather.2

commit v2 on v1

--- a/solution.py
+++ b/solution.py
@@ -132,23 +132,22 @@
     return (base, (mixed, attn_kept, norm_back))
 
 
-def self_backward(d_base, kept, states, weights):
-    mixed, attn_kept, norm_back = kept
+def self_mix_backward(d_base, kept, weights):
+    mixed, _, norm_back = kept
     d_pre, d_gain, d_bias = norm_back(d_base)
     d_branch = d_pre.astype(jnp.bfloat16)
     grad_self_output = weight_grad(mixed, d_branch)
     d_mixed = matmul_back(d_branch, weights[10]).astype(jnp.bfloat16)
-    d_query, d_kv = attend_back(d_mixed, attn_kept)
-    d_qkv = jnp.concatenate([d_query, d_kv], axis=-1)
-    grad_self_qkv = weight_grad(states, d_qkv)
-    d_states = d_pre + matmul_back(d_qkv, weights[9])
-    return (d_states, (grad_self_qkv, grad_self_output, d_gain, d_bias))
-
-
-def stream_forward(base, low_base, weights, key_values, live):
+    return (d_pre, d_mixed, grad_self_output, (d_gain, d_bias))
+
+
+def cross_forward(low_base, weights, key_values, live):
     inner = weights[0].shape[1]
     query = matmul(low_base, weights[0]).astype(jnp.bfloat16)
-    mixed, attn_kept = attend(query, key_values[..., :inner], key_values[..., inner:], live, HEADS)
+    return attend(query, key_values[..., :inner], key_values[..., inner:], live, HEADS)
+
+
+def stream_forward(base, mixed, weights):
     branch = matmul(mixed, weights[2])
     norm_values = tuple((piece.astype(jnp.float32) for piece in weights[5:9]))
     hidden, first_norm = jax.vjp(layer_norm, base + branch, norm_values[0], norm_values[1])
@@ -158,36 +157,26 @@
     result, second_norm = jax.vjp(
         layer_norm, hidden + matmul(low_active, weights[4]), norm_values[2], norm_values[3]
     )
-    kept = (low_base, mixed, attn_kept, first_norm, low_hidden, gelu_back, low_active, second_norm)
-    return (result, kept)
-
-
-def stream_backward(d_result, kept, weights):
-    low_base, mixed, attn_kept, first_norm, low_hidden, gelu_back, low_active, second_norm = kept
+    return (result, (first_norm, low_hidden, gelu_back, low_active, second_norm))
+
+
+def feed_backward(d_result, kept, weights):
+    _, low_hidden, gelu_back, low_active, second_norm = kept
     d_raw, d_gain_two, d_bias_two = second_norm(d_result)
     d_down_in = d_raw.astype(jnp.bfloat16)
     grad_down = weight_grad(low_active, d_down_in)
     d_gate = gelu_back(matmul_back(d_down_in, weights[4]))[0].astype(jnp.bfloat16)
     grad_up = weight_grad(low_hidden, d_gate)
     d_hidden = d_raw + matmul_back(d_gate, weights[3])
-    d_sum, d_gain_one, d_bias_one = first_norm(d_hidden)
+    return (d_hidden, grad_up, grad_down, (d_gain_two, d_bias_two))
+
+
+def mix_backward(d_hidden, mixed, kept, weights):
+    d_sum, d_gain_one, d_bias_one = kept[0](d_hidden)
     d_branch = d_sum.astype(jnp.bfloat16)
     grad_output = weight_grad(mixed, d_branch)
     d_mixed = matmul_back(d_branch, weights[2]).astype(jnp.bfloat16)
-    d_query, d_kv = attend_back(d_mixed, attn_kept)
-    grad_query = weight_grad(low_base, d_query)
-    d_base = d_sum + matmul_back(d_query, weights[0])
-    grads = (
-        grad_query,
-        grad_output,
-        grad_up,
-        grad_down,
-        d_gain_one,
-        d_bias_one,
-        d_gain_two,
-        d_bias_two,
-    )
-    return (d_base, d_kv, grads)
+    return (d_sum, d_mixed, grad_output, (d_gain_one, d_bias_one))
 
 
 def lane_slabs(piece, width):
@@ -215,6 +204,10 @@
 
 
 def gather_pack(groups, vectors=()):
+    return gather_cut(gather_whole(groups, vectors), groups, vectors)
+
+
+def gather_whole(groups, vectors=()):
     parts = []
     for group in groups:
         joined = jnp.concatenate(group, axis=1)
@@ -225,7 +218,11 @@
     packed = jnp.concatenate(parts, axis=0)
     whole = lax.all_gather(packed, ALL, axis=0, tiled=True)
     shards = whole.shape[0] // packed.shape[0]
-    whole = whole.reshape(shards, packed.shape[0], WIDTH)
+    return whole.reshape(shards, packed.shape[0], WIDTH)
+
+
+def gather_cut(whole, groups, vectors=()):
+    shards = whole.shape[0]
     full = []
     at = 0
     for group in groups:
@@ -255,7 +252,7 @@
     return keep.astype(jnp.float32) + got.astype(jnp.float32)
 
 
-def scatter_pack(groups, width, stream_first, vectors=()):
+def scatter_pack(groups, width, vectors=()):
     shards = lax.axis_size(ALL)
     bits = lax.axis_size("batch").bit_length() - 1
     parts = []
@@ -268,12 +265,21 @@
         lines = [vector.reshape(shards, -1) for vector in vectors]
         parts.append(vector_rows(lines, width).astype(jnp.bfloat16))
     block = jnp.concatenate(parts, axis=1)
-    block = block.reshape((2,) * (bits + 1) + block.shape[1:])
+    return block.reshape((2,) * (bits + 1) + block.shape[1:])
+
+
+def reduce_steps(block, stream_first, begin, end=None):
+    bits = lax.axis_size("batch").bit_length() - 1
     order = [("batch", bit) for bit in range(bits)]
     order.insert(1 if stream_first else 2, ("stream", 0))
-    for axis, bit in order:
+    for axis, bit in order[begin:end]:
         place = 0 if axis == "stream" else bits - bit
         block = halve(block.astype(jnp.bfloat16), place, axis, bit)
+    return block if end is None else block.astype(jnp.bfloat16)
+
+
+def scatter_cut(block, groups, width, vectors=()):
+    shards = lax.axis_size(ALL)
     own = block.reshape(block.shape[-2:])
     result = []
     at = 0
@@ -353,11 +359,10 @@
             image_norm0_bias,
         ),
     )
-    out_t, up_t, down_t, out_i, up_i, down_i = gather_pack(
-        ((text_output,), (text_up,), (text_down,), (image_output, image_up, image_down))
-    )
-    text_weights = (qt, kvt, out_t, up_t, down_t, *norms[:4], qkv_t, so_t, *norms[4:6])
-    image_weights = (qi, kvi, out_i, up_i, down_i, *norms[6:10], qkv_i, so_i, *norms[10:])
+    later = ((text_output,), (text_up,), (text_down,), (image_output, image_up, image_down))
+    whole = gather_whole(later)
+    text_weights = (qt, kvt, None, None, None, *norms[:4], qkv_t, so_t, *norms[4:6])
+    image_weights = (qi, kvi, None, None, None, *norms[6:10], qkv_i, so_i, *norms[10:])
     width = image_states.shape[2]
     pairs = text_states.shape[0]
     slots = text_states.shape[1]
@@ -372,48 +377,111 @@
     low_image = image_base.astype(jnp.bfloat16)
     text_kv = matmul(low_text, text_weights[1]).astype(jnp.bfloat16)
     image_kv = matmul(low_image, image_weights[1]).astype(jnp.bfloat16)
-    text_result, text_kept = stream_forward(
-        text_base, low_text, text_weights, image_kv, region_live
-    )
-    image_result, image_kept = stream_forward(
-        image_base, low_image, image_weights, text_kv, text_live
-    )
+    text_mixed, text_attn = cross_forward(low_text, text_weights, image_kv, region_live)
+    image_mixed, image_attn = cross_forward(low_image, image_weights, text_kv, text_live)
+    whole, text_mixed, image_mixed = lax.optimization_barrier((whole, text_mixed, image_mixed))
+    out_t, up_t, down_t, out_i, up_i, down_i = gather_cut(whole, later)
+    text_weights = (*text_weights[:2], out_t, up_t, down_t, *text_weights[5:])
+    image_weights = (*image_weights[:2], out_i, up_i, down_i, *image_weights[5:])
+    text_result, text_kept = stream_forward(text_base, text_mixed, text_weights)
+    image_result, image_kept = stream_forward(image_base, image_mixed, image_weights)
     image_result = partner(image_result.astype(jnp.bfloat16), "stream", 0)
-    d_text_base, d_image_kv, text_grads = stream_backward(
+
+    d_text, text_up_grad, text_down_grad, text_two = feed_backward(
         text_cotangent.astype(jnp.float32), text_kept, text_weights
     )
-    d_image_base, d_text_kv, image_grads = stream_backward(
+    d_image, image_up_grad, image_down_grad, image_two = feed_backward(
         image_cotangent.astype(jnp.float32), image_kept, image_weights
     )
-    up_text, down_text = scatter_pack(((text_grads[2],), (text_grads[3],)), WIDTH, False)
-    up_image, down_image = scatter_pack(((image_grads[2],), (image_grads[3],)), width, True)
+    text_a = ((text_up_grad,), (text_down_grad,))
+    image_a = ((image_up_grad,), (image_down_grad,))
+    sum_ta = scatter_pack(text_a, WIDTH)
+    sum_ia = scatter_pack(image_a, width)
+    d_text, d_image, sum_ta, sum_ia = lax.optimization_barrier((d_text, d_image, sum_ta, sum_ia))
+    sum_ta = reduce_steps(sum_ta, False, 0, 1)
+    sum_ia = reduce_steps(sum_ia, True, 0, 1)
+
+    d_text_sum, d_text_mixed, text_output_grad, text_one = mix_backward(
+        d_text, text_mixed, text_kept, text_weights
+    )
+    d_image_sum, d_image_mixed, image_output_grad, image_one = mix_backward(
+        d_image, image_mixed, image_kept, image_weights
+    )
+    d_text_mixed, d_image_mixed, sum_ta, sum_ia = lax.optimization_barrier(
+        (d_text_mixed, d_image_mixed, sum_ta, sum_ia)
+    )
+    sum_ta = reduce_steps(sum_ta, False, 1, 2)
+    sum_ia = reduce_steps(sum_ia, True, 1, 2)
+
+    d_text_query, d_image_kv = attend_back(d_text_mixed, text_attn)
+    d_image_query, d_text_kv = attend_back(d_image_mixed, image_attn)
+    text_query_grad = weight_grad(low_text, d_text_query)
+    image_query_grad = weight_grad(low_image, d_image_query)
     text_kv_grad = weight_grad(low_text, d_text_kv)
     image_kv_grad = weight_grad(low_image, d_image_kv)
-    output_text, query_text, kv_text = scatter_pack(
-        ((text_grads[1],), (text_grads[0], text_kv_grad)), WIDTH, False
-    )
-    output_image, query_image, kv_image = scatter_pack(
-        ((image_grads[1],), (image_grads[0],), (image_kv_grad,)), width, True
-    )
-    d_text_base = d_text_base + matmul_back(d_text_kv, text_weights[1])
-    d_image_base = d_image_base + matmul_back(d_image_kv, image_weights[1])
-    d_text, text_self_grads = self_backward(d_text_base, text_self_kept, text_states, text_weights)
-    d_image, image_self_grads = self_backward(
-        d_image_base, image_self_kept, image_states, image_weights
-    )
-    d_image = partner(d_image, "stream", 0)
-    qkv_text, so_text, *text_vectors = scatter_pack(
-        ((text_self_grads[0],), (text_self_grads[1],)),
-        WIDTH,
-        False,
-        (*text_grads[4:8], *text_self_grads[2:4]),
-    )
-    qkv_image, so_image, *image_vectors = scatter_pack(
-        ((image_self_grads[0],), (image_self_grads[1],)),
-        width,
-        True,
-        (*image_grads[4:8], *image_self_grads[2:4]),
-    )
+    d_text = (
+        d_text_sum
+        + matmul_back(d_text_query, text_weights[0])
+        + matmul_back(d_text_kv, text_weights[1])
+    )
+    d_image = (
+        d_image_sum
+        + matmul_back(d_image_query, image_weights[0])
+        + matmul_back(d_image_kv, image_weights[1])
+    )
+    text_b = ((text_output_grad,), (text_query_grad, text_kv_grad))
+    image_b = ((image_output_grad,), (image_query_grad,), (image_kv_grad,))
+    sum_tb = scatter_pack(text_b, WIDTH)
+    sum_ib = scatter_pack(image_b, width)
+    d_text, d_image, sum_tb, sum_ib, sum_ta, sum_ia = lax.optimization_barrier(
+        (d_text, d_image, sum_tb, sum_ib, sum_ta, sum_ia)
+    )
+    sum_ta = reduce_steps(sum_ta, False, 2, 3)
+    sum_ia = reduce_steps(sum_ia, True, 2, 3)
+    sum_tb = reduce_steps(sum_tb, False, 0, 1)
+    sum_ib = reduce_steps(sum_ib, True, 0, 1)
+
+    d_text_pre, d_text_self, text_so_grad, text_zero = self_mix_backward(
+        d_text, text_self_kept, text_weights
+    )
+    d_image_pre, d_image_self, image_so_grad, image_zero = self_mix_backward(
+        d_image, image_self_kept, image_weights
+    )
+    d_text_self, d_image_self, sum_tb, sum_ib = lax.optimization_barrier(
+        (d_text_self, d_image_self, sum_tb, sum_ib)
+    )
+    sum_tb = reduce_steps(sum_tb, False, 1, 2)
+    sum_ib = reduce_steps(sum_ib, True, 1, 2)
+
+    d_image_qkv = jnp.concatenate(attend_back(d_image_self, image_self_kept[1]), axis=-1)
+    d_text_qkv = jnp.concatenate(attend_back(d_text_self, text_self_kept[1]), axis=-1)
+    image_qkv_grad = weight_grad(image_states, d_image_qkv)
+    text_qkv_grad = weight_grad(text_states, d_text_qkv)
+    text_vectors = (*text_one, *text_two, *text_zero)
+    image_vectors = (*image_one, *image_two, *image_zero)
+    text_c = ((text_qkv_grad,), (text_so_grad,))
+    image_c = ((image_qkv_grad,), (image_so_grad,))
+    sum_tc = scatter_pack(text_c, WIDTH, text_vectors)
+    sum_ic = scatter_pack(image_c, width, image_vectors)
+    d_text_qkv, d_image_qkv, sum_tc, sum_ic, sum_ta, sum_ia = lax.optimization_barrier(
+        (d_text_qkv, d_image_qkv, sum_tc, sum_ic, sum_ta, sum_ia)
+    )
+    sum_tc = reduce_steps(sum_tc, False, 0, 1)
+    sum_ic = reduce_steps(sum_ic, True, 0, 1)
+    d_image = partner(d_image_pre + matmul_back(d_image_qkv, image_weights[9]), "stream", 0)
+    d_text = d_text_pre + matmul_back(d_text_qkv, text_weights[9])
+    sum_tc = reduce_steps(sum_tc, False, 1)
+    sum_ic = reduce_steps(sum_ic, True, 1)
+    sum_tb = reduce_steps(sum_tb, False, 2)
+    sum_ib = reduce_steps(sum_ib, True, 2)
+    sum_ta = reduce_steps(sum_ta, False, 3)
+    sum_ia = reduce_steps(sum_ia, True, 3)
+    up_text, down_text = scatter_cut(sum_ta, text_a, WIDTH)
+    up_image, down_image = scatter_cut(sum_ia, image_a, width)
+    output_text, query_text, kv_text = scatter_cut(sum_tb, text_b, WIDTH)
+    output_image, query_image, kv_image = scatter_cut(sum_ib, image_b, width)
+    qkv_text, so_text, *text_vectors = scatter_cut(sum_tc, text_c, WIDTH, text_vectors)
+    qkv_image, so_image, *image_vectors = scatter_cut(sum_ic, image_c, width, image_vectors)
     return (
         text_result.astype(jnp.bfloat16),
         image_result,

time: 956 us -> 866 us (0.906)
  waiting for transfers between devices: 480 us -> 368 us
  other arithmetic: 72.5 us -> 92.6 us
    ppermute x30, waiting for transfers between devices: 231 us -> 169 us  [halve(): got = lax.ppermute(give, axis, route)]
    all_gather x2, waiting for transfers between devices: 234 us -> 195 us  [gather_whole(): whole = lax.all_gather(packed, ALL, axis=0, tiled=True)]
    ppermute x5, waiting for transfers between devices: 15.8 us -> 4.97 us  [partner(): return lax.ppermute(block, axis, route)]
    dynamic_slice x29 -> x30, local copies, waits for them, and re-layouts: 18.7 us -> 29 us  [halve(): give = lax.dynamic_index_in_dim(block, 1 - mine, axis=place)]
    unnamed x494 -> x486, local copies, waits for them, and re-layouts: 52.5 us -> 50.2 us
  transfers between devices with their start and end apart: 37 -> 37, of which waited for: 20 -> 22; matrix products, arithmetic and copies ran while one was open for 18% -> 30% of each run, Pallas kernels for 0% -> 0%
where the time goes in v2:
time: 866 us; the launch traced here: 856 us
  waiting for transfers between devices  368 us (42%)
  local copies, waits for them, and re-layouts  184 us (21%)
  matrix products  162 us (19%)
  other arithmetic  92.6 us (11%)
  starting transfers between devices  31.5 us (4%)
  between operations  17.6 us (2%)
    all_gather x2, waiting for transfers between devices, gather_whole(): whole = lax.all_gather(packed, ALL, axis=0, tiled=True)  195 us
    ppermute x30, waiting for transfers between devices, halve(): got = lax.ppermute(give, axis, route)  169 us
    unnamed x486, local copies, waits for them, and re-layouts  50.2 us
    dot_general x14, matrix products, matmul_back(): jnp.einsum('psn,wn->psw', grad, weight, preferred_element_type=jnp.float32)  43.8 us
    dot_general x14, matrix products, weight_grad(): jnp.einsum('psw,psn->wn', inputs, grad, preferred_element_type=jnp.float32)  37.6 us
    convert_element_type x12, other arithmetic, reduce_steps(): return block if end is None else block.astype(jnp.bfloat16)  35.5 us
    slice x5, local copies, waits for them, and re-layouts, gather_cut(): slabs.append(whole[:, at:at + rows].reshape(shards * rows, WIDTH))  33.8 us
    dot_general x14, matrix products, matmul(): return jnp.dot(left, right, preferred_element_type=jnp.float32)  32.2 us
  transfers between devices with their start and end apart: 37, of which 22 were waited for; matrix products, arithmetic and copies ran while one was open for 30% of the time, Pallas kernels for 0%

profile of v2, /device:TPU:0, one launch (start us, length us, event | category | flops | bytes accessed | tf_op | source)
XLA Modules:
  0.0 856.0 jit_solution(16887426441455450831)
XLA Ops:
  7.3 8.2 concatenate.187
  38.5 153.9 %all-gather.3.cloned.1.call-done = bf16[16640,768]{1,0:T(8,128)(2,1)} async-done(((bf16[520,768]{1,0:T(8,128)(2,1)}), bf16[16640,768]{1,0:T(8,128)(2,1)}) %all-gather.3.cloned.1.call-update) | async-done | bytes 25559056 | tf_op jit(solution)/shard_map/all_gather | solution.py:219
  193.5 11.1 %fusion.241 = (bf16[32,32,768]{2,1,0:T(8,128)(2,1)S(1)}, bf16[32,32,768]{2,1,0:T(8,128)(2,1)}, bf16[32,32,768]{2,1,0:T(8,128)(2,1)}, bf16[32,32,768]{2,1,0:T(8,1...) fusion(bf16[32,520,768]{2,1,0:T(8,128)(2,1)} %bitcast.390), kind=kLoop, calls=%fused_computation.519 | loop fusion | bytes 31457280 | tf_op jit(solution)/shard_map/slice | solution.py:233
  222.2 7.1 fusion.242
  270.2 40.6 %all-gather.5.cloned.1.call-done = bf16[11264,768]{1,0:T(8,128)(2,1)} async-done(((bf16[352,768]{1,0:T(8,128)(2,1)}), bf16[11264,768]{1,0:T(8,128)(2,1)}) %all-gather.5.cloned.1.call-update) | async-done | bytes 17301520 | tf_op jit(solution)/shard_map/all_gather | solution.py:219
  320.4 6.2 fusion.243
  338.0 14.2 %multiply_convert_fusion = (bf16[4,128,3072]{2,1,0:T(8,128)(2,1)S(1)}, f32[4,128,3072]{2,1,0:T(8,128)S(1)}) fusion(f32[4,128,3072]{2,1,0:T(8,128)S(1)} %get-tuple-element.327, u8[128,3072]{1,0:T(8,128)(4,1)S(1)} %get-tuple-element.175, u8[128,3072]{1,0:T(8,128)(4,1)S(1)} %get-tuple-element.174), kind=kLoop, calls=%fused_computation.24 | loop fusion | flops 110100480 | bytes 16515072 | tf_op jit(solution)/shard_map/convert_element_type | solution.py:156
  363.3 8.0 add_convert_fusion.4
  371.3 7.5 add_add_fusion.5
  435.9 6.7 add_convert_fusion
  512.0 29.1 %collective-permute-done.6 = bf16[2,2,2,1,1,192,768]{6,5,4,3,2,1,0:T(8,128)(2,1)S(1)} collective-permute-done((bf16[2,2,2,1,1,192,768]{6,5,4,3,2,1,0:T(8,128)(2,1)S(1)}, bf16[2,2,2,1,1,192,768]{6,5,4,3,2,1,0:T(8,128)(2,1)S(1)}, u32[]{:S(2)}, u32[]{:S(2)}) %collective-permute-start.6) | collective-permute-done | bytes 2359328 | tf_op jit(solution)/shard_map/ppermute | solution.py:251
  570.6 7.6 collective-permute-done.11
  579.2 7.2 collective-permute-done.10
  592.2 6.4 add_convert_fusion.2
  676.7 5.6 collective-permute-done.28
  683.4 9.1 %collective-permute-done.17 = bf16[1,2,1,1,1,192,768]{6,5,4,3,2,1,0:T(8,128)(2,1)S(1)} collective-permute-done((bf16[1,2,1,1,1,192,768]{6,5,4,3,2,1,0:T(8,128)(2,1)S(1)}, bf16[1,2,1,1,1,192,768]{6,5,4,3,2,1,0:T(8,128)(2,1)S(1)}, u32[]{:S(2)}, u32[]{:S(2)}) %collective-permute-start.17) | collective-permute-done | bytes 589856 | tf_op jit(solution)/shard_map/ppermute | solution.py:251
  694.2 9.8 %collective-permute-done.29 = bf16[1,1,1,1,1,64,1024]{6,5,4,3,2,1,0:T(8,128)(2,1)S(1)} collective-permute-done((bf16[1,1,1,1,1,64,1024]{6,5,4,3,2,1,0:T(8,128)(2,1)S(1)}, bf16[1,1,1,1,1,64,1024]{6,5,4,3,2,1,0:T(8,128)(2,1)S(1)}, u32[]{:S(2)}, u32[]{:S(2)}) %collective-permute-start.29) | collective-permute-done | bytes 131104 | tf_op jit(solution)/shard_map/ppermute | solution.py:251
  721.9 10.6 %collective-permute-done.14 = bf16[1,2,2,1,1,128,768]{6,5,4,3,2,1,0:T(8,128)(2,1)S(1)} collective-permute-done((bf16[1,2,2,1,1,128,768]{6,5,4,3,2,1,0:T(8,128)(2,1)S(1)}, bf16[1,2,2,1,1,128,768]{6,5,4,3,2,1,0:T(8,128)(2,1)S(1)}, u32[]{:S(2)}, u32[]{:S(2)}) %collective-permute-start.14) | collective-permute-done | bytes 786464 | tf_op jit(solution)/shard_map/ppermute | solution.py:251
  756.9 13.9 %collective-permute-done.20 = bf16[2,2,2,1,1,104,768]{6,5,4,3,2,1,0:T(8,128)(2,1)S(1)} collective-permute-done((bf16[2,2,2,1,1,104,768]{6,5,4,3,2,1,0:T(8,128)(2,1)S(1)}, bf16[2,2,2,1,1,104,768]{6,5,4,3,2,1,0:T(8,128)(2,1)S(1)}, u32[]{:S(2)}, u32[]{:S(2)}) %collective-permute-start.20) | collective-permute-done | bytes 1277984 | tf_op jit(solution)/shard_map/ppermute | solution.py:251
  774.4 26.8 %collective-permute-done.31 = bf16[1,2,2,2,1,136,1024]{6,5,4,3,2,1,0:T(8,128)(2,1)S(1)} collective-permute-done((bf16[1,2,2,2,1,136,1024]{6,5,4,3,2,1,0:T(8,128)(2,1)S(1)}, bf16[1,2,2,2,1,136,1024]{6,5,4,3,2,1,0:T(8,128)(2,1)S(1)}, u32[]{:S(2)}, u32[]{:S(2)}) %collective-permute-start.31) | collective-permute-done | bytes 2228256 | tf_op jit(solution)/shard_map/ppermute | solution.py:251
  803.4 8.2 collective-permute-done.21
  812.6 7.0 collective-permute-done.22
  828.2 6.8 collective-permute-done.33
  837.1 8.7 %collective-permute-done.34 = bf16[1,1,1,1,1,136,1024]{6,5,4,3,2,1,0:T(8,128)(2,1)S(1)} collective-permute-done((bf16[1,1,1,1,1,136,1024]{6,5,4,3,2,1,0:T(8,128)(2,1)S(1)}, bf16[1,1,1,1,1,136,1024]{6,5,4,3,2,1,0:T(8,128)(2,1)S(1)}, u32[]{:S(2)}, u32[]{:S(2)}) %collective-permute-start.34) | collective-permute-done | bytes 278560 | tf_op jit(solution)/shard_map/ppermute | solution.py:251
  (839 shorter events, 418.1 us)
Async XLA Ops:
  7.3 185.1 %all-gather.3.cloned.1.call-start = ((), (), s32[]{:S(2)}) async-start(), calls=%async_computation | async-start | bytes 26357760 | tf_op jit(solution)/shard_map/all_gather | solution.py:219
  30.7 280.2 %all-gather.5.cloned.1.call-start = ((), (), s32[]{:S(2)}) async-start(), calls=%async_computation.1 | async-start | bytes 17842176 | tf_op jit(solution)/shard_map/all_gather | solution.py:219
  35.7 352.0 %collective-permute-start.3 = (bf16[4,36,1024]{2,1,0:T(8,128)(2,1)}, bf16[4,36,1024]{2,1,0:T(8,128)(2,1)}, u32[]{:S(2)}, u32[]{:S(2)}) collective-permute-start(bf16[4,36,1024]{2,1,0:T(8,128)(2,1)} %copy.225), channel_id=1, source_target_pairs={{0,16},{16,0},{1,17},{17,1},{2,18},{18,2},{3,19},{19,3},{4,20},{20... | collective-permute-start | bytes 884744 | tf_op jit(solution)/shard_map/ppermute | solution.py:26
  35.8 170.7 %collective-permute-start = (bf16[4,36,1024]{2,1,0:T(8,128)(2,1)S(1)}, bf16[4,36,1024]{2,1,0:T(8,128)(2,1)S(1)}, u32[]{:S(2)}, u32[]{:S(2)}) collective-permute-start(bf16[4,36,1024]{2,1,0:T(8,128)(2,1)S(1)} %copy.203), channel_id=1, source_target_pairs={{0,16},{16,0},{1,17},{17,1},{2,18},{18,2},{3,19},{19,3},{4,20},{20... | collective-permute-start | bytes 884744 | tf_op jit(solution)/shard_map/ppermute | solution.py:26
  410.8 25.1 %collective-permute-start.4 = (bf16[2,2,2,2,1,192,768]{6,5,4,3,2,1,0:T(8,128)(2,1)}, bf16[2,2,2,2,1,192,768]{6,5,4,3,2,1,0:T(8,128)(2,1)}, u32[]{:S(2)}, u32[]{:S(2)}) collective-permute-start(bf16[2,2,2,2,1,192,768]{6,5,4,3,2,1,0:T(8,128)(2,1)} %constant_dynamic-slice_fusion.29), channel_id=1, source_target_pairs={{0,1},{1,0},{2,3},{3,2},{4,5},{5,4},{6,7},{7,6},{8,9},{9,8},{10,11... | collective-permute-start | bytes 14155784 | tf_op jit(solution)/shard_map/ppermute | solution.py:251
  415.7 17.5 %collective-permute-start.5 = (bf16[2,2,2,2,1,64,1024]{6,5,4,3,2,1,0:T(8,128)(2,1)}, bf16[2,2,2,2,1,64,1024]{6,5,4,3,2,1,0:T(8,128)(2,1)}, u32[]{:S(2)}, u32[]{:S(2)}) collective-permute-start(bf16[2,2,2,2,1,64,1024]{6,5,4,3,2,1,0:T(8,128)(2,1)} %constant_dynamic-slice_fusion.28), channel_id=1, source_target_pairs={{0,1},{1,0},{2,3},{3,2},{4,5},{5,4},{6,7},{7,6},{8,9},{9,8},{10,11... | collective-permute-start | bytes 6291464 | tf_op jit(solution)/shard_map/ppermute | solution.py:251
  485.5 25.1 %collective-permute-start.7 = (bf16[1,2,2,2,1,64,1024]{6,5,4,3,2,1,0:T(8,128)(2,1)S(1)}, bf16[1,2,2,2,1,64,1024]{6,5,4,3,2,1,0:T(8,128)(2,1)S(1)}, u32[]{:S(2)}, u32[]{:S(2)}) collective-permute-start(bf16[1,2,2,2,1,64,1024]{6,5,4,3,2,1,0:T(8,128)(2,1)S(1)} %constant_dynamic-slice_fusion.26), channel_id=1, source_target_pairs={{0,16},{16,0},{1,17},{17,1},{2,18},{18,2},{3,19},{19,3},{4,20},{20... | collective-permute-start | bytes 3145736 | tf_op jit(solution)/shard_map/ppermute | solution.py:251
  488.3 52.8 %collective-permute-start.6 = (bf16[2,2,2,1,1,192,768]{6,5,4,3,2,1,0:T(8,128)(2,1)S(1)}, bf16[2,2,2,1,1,192,768]{6,5,4,3,2,1,0:T(8,128)(2,1)S(1)}, u32[]{:S(2)}, u32[]{:S(2)}) collective-permute-start(bf16[2,2,2,1,1,192,768]{6,5,4,3,2,1,0:T(8,128)(2,1)S(1)} %constant_dynamic-slice_fusion.27), channel_id=1, source_target_pairs={{0,2},{1,3},{2,0},{3,1},{4,6},{5,7},{6,4},{7,5},{8,10},{9,11},{10,... | collective-permute-start | bytes 7077896 | tf_op jit(solution)/shard_map/ppermute | solution.py:251
  549.9 39.2 %collective-permute-start.8 = (bf16[2,2,2,2,1,128,768]{6,5,4,3,2,1,0:T(8,128)(2,1)}, bf16[2,2,2,2,1,128,768]{6,5,4,3,2,1,0:T(8,128)(2,1)}, u32[]{:S(2)}, u32[]{:S(2)}) collective-permute-start(bf16[2,2,2,2,1,128,768]{6,5,4,3,2,1,0:T(8,128)(2,1)} %constant_dynamic-slice_fusion.25), channel_id=1, source_target_pairs={{0,1},{1,0},{2,3},{3,2},{4,5},{5,4},{6,7},{7,6},{8,9},{9,8},{10,11... | collective-permute-start | bytes 9437192 | tf_op jit(solution)/shard_map/ppermute | solution.py:251
  554.8 37.4 %collective-permute-start.9 = (bf16[2,2,2,2,1,128,1024]{6,5,4,3,2,1,0:T(8,128)(2,1)}, bf16[2,2,2,2,1,128,1024]{6,5,4,3,2,1,0:T(8,128)(2,1)}, u32[]{:S(2)}, u32[]{:S(2)}) collective-permute-start(bf16[2,2,2,2,1,128,1024]{6,5,4,3,2,1,0:T(8,128)(2,1)} %constant_dynamic-slice_fusion.24), channel_id=1, source_target_pairs={{0,1},{1,0},{2,3},{3,2},{4,5},{5,4},{6,7},{7,6},{8,9},{9,8},{10,11... | collective-permute-start | bytes 12582920 | tf_op jit(solution)/shard_map/ppermute | solution.py:251
  558.1 28.3 %collective-permute-start.10 = (bf16[1,2,2,1,1,192,768]{6,5,4,3,2,1,0:T(8,128)(2,1)}, bf16[1,2,2,1,1,192,768]{6,5,4,3,2,1,0:T(8,128)(2,1)}, u32[]{:S(2)}, u32[]{:S(2)}) collective-permute-start(bf16[1,2,2,1,1,192,768]{6,5,4,3,2,1,0:T(8,128)(2,1)} %constant_dynamic-slice_fusion.23), channel_id=1, source_target_pairs={{0,16},{16,0},{1,17},{17,1},{2,18},{18,2},{3,19},{19,3},{4,20},{20... | collective-permute-start | bytes 3538952 | tf_op jit(solution)/shard_map/ppermute | solution.py:251
  645.2 68.2 %collective-permute-start.13 = (bf16[2,2,2,1,1,128,768]{6,5,4,3,2,1,0:T(8,128)(2,1)}, bf16[2,2,2,1,1,128,768]{6,5,4,3,2,1,0:T(8,128)(2,1)}, u32[]{:S(2)}, u32[]{:S(2)}) collective-permute-start(bf16[2,2,2,1,1,128,768]{6,5,4,3,2,1,0:T(8,128)(2,1)} %constant_dynamic-slice_fusion.21), channel_id=1, source_target_pairs={{0,2},{1,3},{2,0},{3,1},{4,6},{5,7},{6,4},{7,5},{8,10},{9,11},{10,... | collective-permute-start | bytes 4718600 | tf_op jit(solution)/shard_map/ppermute | solution.py:251
  649.6 67.6 %collective-permute-start.24 = (bf16[1,2,2,2,1,128,1024]{6,5,4,3,2,1,0:T(8,128)(2,1)}, bf16[1,2,2,2,1,128,1024]{6,5,4,3,2,1,0:T(8,128)(2,1)}, u32[]{:S(2)}, u32[]{:S(2)}) collective-permute-start(bf16[1,2,2,2,1,128,1024]{6,5,4,3,2,1,0:T(8,128)(2,1)} %constant_dynamic-slice_fusion.10), channel_id=1, source_target_pairs={{0,16},{16,0},{1,17},{17,1},{2,18},{18,2},{3,19},{19,3},{4,20},{20... | collective-permute-start | bytes 6291464 | tf_op jit(solution)/shard_map/ppermute | solution.py:251
  673.8 18.7 %collective-permute-start.17 = (bf16[1,2,1,1,1,192,768]{6,5,4,3,2,1,0:T(8,128)(2,1)S(1)}, bf16[1,2,1,1,1,192,768]{6,5,4,3,2,1,0:T(8,128)(2,1)S(1)}, u32[]{:S(2)}, u32[]{:S(2)}) collective-permute-start(bf16[1,2,1,1,1,192,768]{6,5,4,3,2,1,0:T(8,128)(2,1)S(1)} %constant_dynamic-slice_fusion.17), channel_id=1, source_target_pairs={{0,4},{1,5},{2,6},{3,7},{4,0},{5,1},{6,2},{7,3},{8,12},{9,13},{10,... | collective-permute-start | bytes 1769480 | tf_op jit(solution)/shard_map/ppermute | solution.py:251
  675.8 69.3 %collective-permute-start.30 = (bf16[2,2,2,2,1,136,1024]{6,5,4,3,2,1,0:T(8,128)(2,1)S(1)}, bf16[2,2,2,2,1,136,1024]{6,5,4,3,2,1,0:T(8,128)(2,1)}, u32[]{:S(2)}, u32[]{:S(2)}) collective-permute-start(bf16[2,2,2,2,1,136,1024]{6,5,4,3,2,1,0:T(8,128)(2,1)S(1)} %constant_dynamic-slice_fusion.4), channel_id=1, source_target_pairs={{0,1},{1,0},{2,3},{3,2},{4,5},{5,4},{6,7},{7,6},{8,9},{9,8},{10,11... | collective-permute-start | bytes 13369352 | tf_op jit(solution)/shard_map/ppermute | solution.py:251
  682.3 26.6 %collective-permute-start.12 = (f32[4,36,1024]{2,0,1:T(4,128)S(1)}, f32[4,36,1024]{2,0,1:T(4,128)S(1)}, u32[]{:S(2)}, u32[]{:S(2)}) collective-permute-start(f32[4,36,1024]{2,0,1:T(4,128)S(1)} %copy.278), channel_id=1, source_target_pairs={{0,16},{16,0},{1,17},{17,1},{2,18},{18,2},{3,19},{19,3},{4,20},{20... | collective-permute-start | bytes 1769480 | tf_op jit(solution)/shard_map/ppermute | solution.py:26
  709.0 24.5 %collective-permute-start.19 = (bf16[2,2,2,2,1,104,768]{6,5,4,3,2,1,0:T(8,128)(2,1)S(1)}, bf16[2,2,2,2,1,104,768]{6,5,4,3,2,1,0:T(8,128)(2,1)S(1)}, u32[]{:S(2)}, u32[]{:S(2)}) collective-permute-start(bf16[2,2,2,2,1,104,768]{6,5,4,3,2,1,0:T(8,128)(2,1)S(1)} %constant_dynamic-slice_fusion.15), channel_id=1, source_target_pairs={{0,1},{1,0},{2,3},{3,2},{4,5},{5,4},{6,7},{7,6},{8,9},{9,8},{10,11... | collective-permute-start | bytes 7667720 | tf_op jit(solution)/shard_map/ppermute | solution.py:251
  715.5 17.1 %collective-permute-start.14 = (bf16[1,2,2,1,1,128,768]{6,5,4,3,2,1,0:T(8,128)(2,1)S(1)}, bf16[1,2,2,1,1,128,768]{6,5,4,3,2,1,0:T(8,128)(2,1)S(1)}, u32[]{:S(2)}, u32[]{:S(2)}) collective-permute-start(bf16[1,2,2,1,1,128,768]{6,5,4,3,2,1,0:T(8,128)(2,1)S(1)} %constant_dynamic-slice_fusion.20), channel_id=1, source_target_pairs={{0,16},{16,0},{1,17},{17,1},{2,18},{18,2},{3,19},{19,3},{4,20},{20... | collective-permute-start | bytes 2359304 | tf_op jit(solution)/shard_map/ppermute | solution.py:251
  720.9 33.6 %collective-permute-start.25 = (bf16[1,2,2,1,1,128,1024]{6,5,4,3,2,1,0:T(8,128)(2,1)}, bf16[1,2,2,1,1,128,1024]{6,5,4,3,2,1,0:T(8,128)(2,1)}, u32[]{:S(2)}, u32[]{:S(2)}) collective-permute-start(bf16[1,2,2,1,1,128,1024]{6,5,4,3,2,1,0:T(8,128)(2,1)} %constant_dynamic-slice_fusion.9), channel_id=1, source_target_pairs={{0,2},{1,3},{2,0},{3,1},{4,6},{5,7},{6,4},{7,5},{8,10},{9,11},{10,... | collective-permute-start | bytes 3145736 | tf_op jit(solution)/shard_map/ppermute | solution.py:251
  734.3 36.5 %collective-permute-start.20 = (bf16[2,2,2,1,1,104,768]{6,5,4,3,2,1,0:T(8,128)(2,1)S(1)}, bf16[2,2,2,1,1,104,768]{6,5,4,3,2,1,0:T(8,128)(2,1)S(1)}, u32[]{:S(2)}, u32[]{:S(2)}) collective-permute-start(bf16[2,2,2,1,1,104,768]{6,5,4,3,2,1,0:T(8,128)(2,1)S(1)} %constant_dynamic-slice_fusion.14), channel_id=1, source_target_pairs={{0,2},{1,3},{2,0},{3,1},{4,6},{5,7},{6,4},{7,5},{8,10},{9,11},{10,... | collective-permute-start | bytes 3833864 | tf_op jit(solution)/shard_map/ppermute | solution.py:251
  749.8 51.4 %collective-permute-start.31 = (bf16[1,2,2,2,1,136,1024]{6,5,4,3,2,1,0:T(8,128)(2,1)S(1)}, bf16[1,2,2,2,1,136,1024]{6,5,4,3,2,1,0:T(8,128)(2,1)S(1)}, u32[]{:S(2)}, u32[]{:S(2)}) collective-permute-start(bf16[1,2,2,2,1,136,1024]{6,5,4,3,2,1,0:T(8,128)(2,1)S(1)} %constant_dynamic-slice_fusion.3), channel_id=1, source_target_pairs={{0,16},{16,0},{1,17},{17,1},{2,18},{18,2},{3,19},{19,3},{4,20},{20... | collective-permute-start | bytes 6684680 | tf_op jit(solution)/shard_map/ppermute | solution.py:251
  771.4 40.2 %collective-permute-start.21 = (bf16[1,2,2,1,1,104,768]{6,5,4,3,2,1,0:T(8,128)(2,1)S(1)}, bf16[1,2,2,1,1,104,768]{6,5,4,3,2,1,0:T(8,128)(2,1)S(1)}, u32[]{:S(2)}, u32[]{:S(2)}) collective-permute-start(bf16[1,2,2,1,1,104,768]{6,5,4,3,2,1,0:T(8,128)(2,1)S(1)} %constant_dynamic-slice_fusion.13), channel_id=1, source_target_pairs={{0,16},{16,0},{1,17},{17,1},{2,18},{18,2},{3,19},{19,3},{4,20},{20... | collective-permute-start | bytes 1916936 | tf_op jit(solution)/shard_map/ppermute | solution.py:251
  772.8 39.0 %collective-permute-start.27 = (bf16[1,1,1,1,1,128,1024]{6,5,4,3,2,1,0:T(8,128)(2,1)S(1)}, bf16[1,1,1,1,1,128,1024]{6,5,4,3,2,1,0:T(8,128)(2,1)S(1)}, u32[]{:S(2)}, u32[]{:S(2)}) collective-permute-start(bf16[1,1,1,1,1,128,1024]{6,5,4,3,2,1,0:T(8,128)(2,1)S(1)} %constant_dynamic-slice_fusion.7), channel_id=1, source_target_pairs={{0,8},{1,9},{2,10},{3,11},{4,12},{5,13},{6,14},{7,15},{8,0},{9,1},... | collective-permute-start | bytes 786440 | tf_op jit(solution)/shard_map/ppermute | solution.py:251
  802.4 19.9 %collective-permute-start.32 = (bf16[1,2,2,1,1,136,1024]{6,5,4,3,2,1,0:T(8,128)(2,1)S(1)}, bf16[1,2,2,1,1,136,1024]{6,5,4,3,2,1,0:T(8,128)(2,1)S(1)}, u32[]{:S(2)}, u32[]{:S(2)}) collective-permute-start(bf16[1,2,2,1,1,136,1024]{6,5,4,3,2,1,0:T(8,128)(2,1)S(1)} %constant_dynamic-slice_fusion.2), channel_id=1, source_target_pairs={{0,2},{1,3},{2,0},{3,1},{4,6},{5,7},{6,4},{7,5},{8,10},{9,11},{10,... | collective-permute-start | bytes 3342344 | tf_op jit(solution)/shard_map/ppermute | solution.py:251
  (230 other events, 2624.0 us)
Sparse Core Ops, SparseCore 0:
  30.8 161.5 all-gather.2
  195.8 114.9 all-gather.4
